TPU v7x, 32 devices: a whole 2x2x4 slice. The times are simulated.
32 devices in a mesh: dp: 4 (over z), row: 4 (over x, core), col: 2 (over y).
Axes of the slice: x: 2, y: 2, z: 4, core: 2. Of those that a mesh axis runs over, the one named last changes fastest.
Arguments:
- hidden: float32 [4096, 1024], P(('dp', 'row')), may hold values from -6 to 6
- cotangent: float32 [4096, 1024], P(('dp', 'row'), 'col'), may hold values from -6 to 6
- norm_gain: float32 [1024], replicated, may hold values from 0.5 to 1.5
- weight_z: bfloat16 [1024, 2048], P('col', 'row'), may hold values from -0.1875 to 0.1875
- weight_x: bfloat16 [1024, 2048], P('col', 'row'), may hold values from -0.1875 to 0.1875
- weight_dt: bfloat16 [1024, 32], P('col', 'row'), may hold values from -0.1875 to 0.1875
- weight_bc: bfloat16 [1024, 256], P('col'), may hold values from -0.1875 to 0.1875
- conv_weight: float32 [4, 2048], P(None, ('row', 'col')), may hold values from -3 to 3
- conv_bias: float32 [2048], P(('row', 'col')), may hold values from -3 to 3
- bc_conv_weight: float32 [4, 256], replicated, may hold values from -3 to 3
- bc_conv_bias: float32 [256], replicated, may hold values from -3 to 3
- dt_bias: float32 [32], P(('row', 'col')), may hold values from -5 to -1
- decay_log: float32 [32], P(('row', 'col')), may hold values from 0 to 2.77
- skip_gain: float32 [32], P(('row', 'col')), may hold values from 0.5 to 1.5
- gate_gain: float32 [2048], P(('row', 'col')), may hold values from 0.25 to 1.75
- out_weight: bfloat16 [2048, 1024], P('row', 'col'), may hold values from -0.125 to 0.125
Outputs:
- output: float32 [4096, 1024], P(('dp', 'row'), 'col')
- grad_hidden: float32 [4096, 1024], P(('dp', 'row'), 'col')
- grad_norm_gain: float32 [1024], P('col')
- grad_weight_z: float32 [1024, 2048], P('col', 'row')
- grad_weight_x: float32 [1024, 2048], P('col', 'row')
- grad_weight_dt: float32 [1024, 32], P('col', 'row')
- grad_weight_bc: float32 [1024, 256], P('col')
- grad_conv_weight: float32 [4, 2048], P(None, ('row', 'col'))
- grad_conv_bias: float32 [2048], P(('row', 'col'))
- grad_bc_conv_weight: float32 [4, 256], replicated
- grad_bc_conv_bias: float32 [256], replicated
- grad_dt_bias: float32 [32], P(('row', 'col'))
- grad_decay_log: float32 [32], P(('row', 'col'))
- grad_skip_gain: float32 [32], P(('row', 'col'))
- grad_gate_gain: float32 [2048], P(('row', 'col'))
- grad_out_weight: float32 [2048, 1024], P('row', 'col')
All inputs are finite; a program needn't handle non-finite values.
Results may differ from a plain program's by a relative error of at most 0.012.
Values may be sent and summed in bfloat16 or wider, within the bound.
A program may use at most 128 MiB of HBM per device.

v0:
```python
import jax
import jax.numpy as jnp
from jax import lax
from jax.sharding import PartitionSpec as P

BLOCK = 256
SEQ_LEN = 1024
INNER = 2048


EPSILON = 1e-05
PRECISE = lax.Precision.HIGHEST


def causal_conv(values, kernel, offset_bias):
    kernel_width = kernel.shape[0]
    length = values.shape[0]
    padded = jnp.pad(values, ((kernel_width - 1, 0), (0, 0)))
    summed = jnp.broadcast_to(offset_bias[None, :], values.shape)
    for offset in range(kernel_width):
        summed = summed + kernel[offset][None, :] * padded[offset : offset + length]
    return summed


def block_scan(inputs, step_sizes, rates, b_values, c_values):
    length, head_count, head_width = inputs.shape
    block_count = length // BLOCK
    state_width = b_values.shape[1]
    blocks = inputs.reshape(block_count, BLOCK, head_count, head_width)
    block_steps = step_sizes.reshape(block_count, BLOCK, head_count)
    log_decay = jnp.cumsum(block_steps * rates[None, None, :], axis=1)
    b_blocks = b_values.reshape(block_count, BLOCK, state_width)
    c_blocks = c_values.reshape(block_count, BLOCK, state_width)
    scores = jnp.einsum("cln,csn->cls", c_blocks, b_blocks, precision=PRECISE)
    causal = jnp.arange(BLOCK)[:, None] >= jnp.arange(BLOCK)[None, :]
    log_gap = log_decay[:, :, None, :] - log_decay[:, None, :, :]
    decays = jnp.exp(jnp.where(causal[None, :, :, None], log_gap, -1e30))
    mixing = scores[:, :, :, None] * decays * block_steps[:, None, :, :]
    inside = jnp.einsum("clsh,cshp->clhp", mixing, blocks, precision=PRECISE)
    tail_decay = jnp.exp(log_decay[:, -1:, :] - log_decay) * block_steps
    states = jnp.einsum("csn,csh,cshp->chpn", b_blocks, tail_decay, blocks, precision=PRECISE)
    carried = jnp.exp(log_decay[:, -1, :])

    def advance(running, pair_item):
        new_state, factor = pair_item
        return (running * factor[:, None, None] + new_state, running)

    initial = jnp.zeros((head_count, head_width, state_width), jnp.float32)
    _, entering = lax.scan(advance, initial, (states, carried))
    outside = jnp.einsum(
        "cln,chpn,clh->clhp", c_blocks, entering, jnp.exp(log_decay), precision=PRECISE
    )
    return (inside + outside).reshape(length, head_count, head_width)


def sequence_mixer(
    z_raw,
    x_raw,
    step_raw,
    bc_raw,
    conv_weight,
    conv_bias,
    bc_conv_weight,
    bc_conv_bias,
    dt_bias,
    decay_log,
    skip_gain,
):
    x_conv = jax.nn.silu(causal_conv(x_raw, conv_weight, conv_bias))
    bc_conv = jax.nn.silu(causal_conv(bc_raw, bc_conv_weight, bc_conv_bias))
    state_width = bc_conv.shape[1] // 2
    head_count = step_raw.shape[1]
    length = x_conv.shape[0]
    heads_in = x_conv.reshape(length, head_count, -1)
    step_size = jax.nn.softplus(step_raw + dt_bias[None, :])
    rates = -jnp.exp(decay_log)
    mixed = block_scan(
        heads_in, step_size, rates, bc_conv[:, :state_width], bc_conv[:, state_width:]
    )
    mixed = mixed + skip_gain[None, :, None] * heads_in
    return mixed.reshape(length, -1) * jax.nn.silu(z_raw)


def group_mixer(
    z_raw,
    x_raw,
    step_raw,
    bc_raw,
    conv_weight,
    conv_bias,
    bc_conv_weight,
    bc_conv_bias,
    dt_bias,
    decay_log,
    skip_gain,
):
    total_rows = z_raw.shape[0]
    seq_count = total_rows // SEQ_LEN

    def split_seqs(matrix):
        return matrix.reshape(seq_count, SEQ_LEN, matrix.shape[1])

    mapped = jax.vmap(
        sequence_mixer, in_axes=(0, 0, 0, 0, None, None, None, None, None, None, None)
    )
    result = mapped(
        split_seqs(z_raw),
        split_seqs(x_raw),
        split_seqs(step_raw),
        split_seqs(bc_raw),
        conv_weight,
        conv_bias,
        bc_conv_weight,
        bc_conv_bias,
        dt_bias,
        decay_log,
        skip_gain,
    )
    return result.reshape(total_rows, -1)


def body(
    hidden,
    cotangent,
    norm_gain,
    weight_z,
    weight_x,
    weight_dt,
    weight_bc,
    conv_weight,
    conv_bias,
    bc_conv_weight,
    bc_conv_bias,
    dt_bias,
    decay_log,
    skip_gain,
    gate_gain,
    out_weight,
):
    row_count = lax.axis_size("row")
    col_count = lax.axis_size("col")
    row_index = lax.axis_index("row")
    col_index = lax.axis_index("col")
    model_width = hidden.shape[1]
    col_width = weight_z.shape[0]
    chan_width = weight_z.shape[1] // col_count
    head_width = weight_dt.shape[1] // col_count
    bc_width = weight_bc.shape[1]
    slot_width = 2 * chan_width + head_width
    inv_rms = lax.rsqrt(jnp.mean(hidden * hidden, axis=1, keepdims=True) + EPSILON)
    normed = hidden * inv_rms
    normed_col = lax.dynamic_slice_in_dim(normed, col_index * col_width, col_width, 1)
    scaled = (normed * norm_gain[None, :]).astype(jnp.bfloat16)
    scaled_col = lax.dynamic_slice_in_dim(scaled, col_index * col_width, col_width, 1)
    gathered_rows = lax.all_gather(scaled_col, "row", axis=0, tiled=True)
    group_rows = gathered_rows.shape[0]
    head_blocks = jnp.concatenate(
        [
            weight_z.reshape(col_width, col_count, chan_width),
            weight_x.reshape(col_width, col_count, chan_width),
            weight_dt.reshape(col_width, col_count, head_width),
        ],
        axis=2,
    ).reshape(col_width, col_count * slot_width)
    with_shared = jnp.concatenate(
        [
            head_blocks.reshape(col_width, col_count, slot_width),
            jnp.broadcast_to(weight_bc[:, None, :], (col_width, col_count, bc_width)),
        ],
        axis=2,
    ).reshape(col_width, col_count * (slot_width + bc_width))
    partial_proj = jnp.dot(gathered_rows, with_shared, preferred_element_type=jnp.float32).reshape(
        group_rows, col_count, slot_width + bc_width
    )
    projected = lax.psum_scatter(partial_proj, "col", scatter_dimension=1, tiled=True).reshape(
        group_rows, slot_width + bc_width
    )
    z_raw = projected[:, :chan_width]
    x_raw = projected[:, chan_width : 2 * chan_width]
    step_raw = projected[:, 2 * chan_width : slot_width]
    bc_raw = projected[:, slot_width:]
    gated, pullback = jax.vjp(
        group_mixer,
        z_raw,
        x_raw,
        step_raw,
        bc_raw,
        conv_weight,
        conv_bias,
        bc_conv_weight,
        bc_conv_bias,
        dt_bias,
        decay_log,
        skip_gain,
    )
    square_total = lax.psum(jnp.sum(gated * gated, axis=1), ("row", "col"))
    inv_gate = lax.rsqrt(square_total[:, None] / INNER + EPSILON)
    gate_hat = gated * inv_gate
    gate_out = (gate_hat * gate_gain[None, :]).astype(jnp.bfloat16)
    gate_rows = lax.all_gather(gate_out, "col", axis=1, tiled=True)
    piece = gate_rows
    branch_out = lax.psum_scatter(
        jnp.dot(piece, out_weight, preferred_element_type=jnp.float32),
        "row",
        scatter_dimension=0,
        tiled=True,
    )
    hidden_col = lax.dynamic_slice_in_dim(hidden, col_index * col_width, col_width, 1)
    output = hidden_col + branch_out
    cot_half = cotangent.astype(jnp.bfloat16)
    cot_rows = lax.all_gather(cot_half, "row", axis=0, tiled=True)
    grad_out_weight = lax.dot_general(
        gate_rows, cot_rows, (((0,), (0,)), ((), ())), preferred_element_type=jnp.float32
    )
    chan_part = lax.dot_general(
        cot_rows, out_weight, (((1,), (1,)), ((), ())), preferred_element_type=jnp.float32
    )
    grad_gate_out = lax.psum_scatter(chan_part, "col", scatter_dimension=1, tiled=True)
    grad_gate_gain = jnp.sum(grad_gate_out * gate_hat, axis=0)
    grad_hat = grad_gate_out * gate_gain[None, :]
    gate_dot = lax.psum(jnp.sum(grad_hat * gate_hat, axis=1), ("row", "col"))
    grad_gated = inv_gate * (grad_hat - gate_hat * (gate_dot[:, None] / INNER))
    (
        grad_z,
        grad_x,
        grad_step,
        grad_bc,
        grad_conv_weight,
        grad_conv_bias,
        grad_bc_conv_weight,
        grad_bc_conv_bias,
        grad_dt_bias,
        grad_decay_log,
        grad_skip_gain,
    ) = pullback(grad_gated)
    bc_total = lax.psum(grad_bc, "col")
    grad_slot = jnp.concatenate([grad_z, grad_x, grad_step], axis=1).astype(jnp.bfloat16)
    grad_cols = lax.all_gather(grad_slot, "col", axis=1, tiled=True)
    bc_wide = weight_bc.astype(jnp.float32)
    piece = grad_cols
    heads_term = lax.dot_general(
        piece, head_blocks, (((1,), (1,)), ((), ())), preferred_element_type=jnp.float32
    )
    grad_scaled = lax.psum_scatter(
        heads_term + jnp.dot(bc_total, bc_wide.T, precision=PRECISE),
        "row",
        scatter_dimension=0,
        tiled=True,
    )
    head_grads = lax.dot_general(
        gathered_rows, grad_cols, (((0,), (0,)), ((), ())), preferred_element_type=jnp.float32
    ).reshape(col_width, col_count, slot_width)
    grad_weight_z = head_grads[:, :, :chan_width].reshape(col_width, col_count * chan_width)
    grad_weight_x = head_grads[:, :, chan_width : 2 * chan_width].reshape(
        col_width, col_count * chan_width
    )
    grad_weight_dt = head_grads[:, :, 2 * chan_width :].reshape(col_width, col_count * head_width)
    bc_part = jnp.dot(gathered_rows.astype(jnp.float32).T, bc_total, precision=PRECISE)
    gain_col = lax.dynamic_slice_in_dim(norm_gain, col_index * col_width, col_width, 0)
    gain_part = jnp.sum(grad_scaled * normed_col, axis=0)
    grad_in = grad_scaled * gain_col[None, :]
    input_dot = jnp.sum(grad_in * normed_col, axis=1)
    row_hot = (jnp.arange(row_count) == row_index).astype(jnp.float32)
    col_hot = (jnp.arange(col_count) == col_index).astype(jnp.float32)
    dot_slots, gain_slots, bc_slots, bc_weight_sum, bc_bias_sum = lax.psum(
        (
            row_hot[:, None] * input_dot[None, :],
            col_hot[:, None] * gain_part[None, :],
            col_hot[:, None, None] * bc_part[None, :, :],
            grad_bc_conv_weight,
            grad_bc_conv_bias,
        ),
        ("row", "col"),
    )
    input_total = lax.dynamic_index_in_dim(dot_slots, row_index, 0, keepdims=False)
    gain_mine = lax.dynamic_index_in_dim(gain_slots, col_index, 0, keepdims=False)
    bc_mine = lax.dynamic_index_in_dim(bc_slots, col_index, 0, keepdims=False)
    grad_hidden = cotangent + inv_rms * (
        grad_in - normed_col * (input_total[:, None] / model_width)
    )
    summed = lax.psum(
        (
            gain_mine,
            grad_weight_z,
            grad_weight_x,
            grad_weight_dt,
            bc_mine,
            grad_conv_weight,
            grad_conv_bias,
            bc_weight_sum,
            bc_bias_sum,
            grad_dt_bias,
            grad_decay_log,
            grad_skip_gain,
            grad_gate_gain,
            grad_out_weight,
        ),
        "dp",
    )
    return (
        output,
        grad_hidden,
        summed[0],
        summed[1],
        summed[2],
        summed[3],
        summed[4],
        summed[5],
        summed[6],
        summed[7],
        summed[8],
        summed[9],
        summed[10],
        summed[11],
        summed[12],
        summed[13],
    )


def solution(mesh):
    in_specs = (
        P(("dp", "row"), None),
        P(("dp", "row"), "col"),
        P(),
        P("col", "row"),
        P("col", "row"),
        P("col", "row"),
        P("col", None),
        P(None, ("row", "col")),
        P(("row", "col")),
        P(),
        P(),
        P(("row", "col")),
        P(("row", "col")),
        P(("row", "col")),
        P(("row", "col")),
        P("row", "col"),
    )
    out_specs = (
        P(("dp", "row"), "col"),
        P(("dp", "row"), "col"),
        P("col"),
        P("col", "row"),
        P("col", "row"),
        P("col", "row"),
        P("col", None),
        P(None, ("row", "col")),
        P(("row", "col")),
        P(),
        P(),
        P(("row", "col")),
        P(("row", "col")),
        P(("row", "col")),
        P(("row", "col")),
        P("row", "col"),
    )
    return jax.shard_map(body, mesh=mesh, in_specs=in_specs, out_specs=out_specs, check_vma=False)
```

profile of v0, /device:TPU:0, one launch (start us, length us, event | category | flops | bytes accessed | tf_op | source)
XLA Modules:
  0.0 656.6 jit_solution(7282166113597032252)
XLA Ops:
  17.7 1.7 dot_general.111
  19.4 11.9 %all-gather.6.cloned.1.call-done = bf16[1024,512]{1,0:T(8,128)(2,1)} async-done(((bf16[256,512]{1,0:T(8,128)(2,1)}), bf16[1024,512]{1,0:T(8,128)(2,1)}) %all-gather.6.cloned.1.call-update) | async-done | bytes 1048592 | tf_op jit(solution)/shard_map/all_gather | solution.py:155
  31.2 5.8 fusion.42
  38.7 11.5 %all-gather.10.cloned.1.call-done = bf16[1024,512]{1,0:T(8,128)(2,1)} async-done(((bf16[256,512]{1,0:T(8,128)(2,1)}), bf16[1024,512]{1,0:T(8,128)(2,1)}) %all-gather.10.cloned.1.call-update) | async-done | bytes 1048592 | tf_op jit(solution)/shard_map/all_gather | solution.py:211
  50.1 3.3 fusion.97
  53.5 76.8 %reduce-scatter.5.cloned.1.call-done = f32[1024,1,772]{0,2,1:T(8,128)} async-done(((f32[1024,2,772]{0,2,1:T(8,128)}), f32[1024,1,772]{0,2,1:T(8,128)}) %reduce-scatter.5.cloned.1.call-update) | async-done | bytes 3162128 | tf_op jit(solution)/shard_map/reduce_scatter | solution.py:175
  131.3 4.8 reduce-window.14
  137.3 2.4 slice_bitcast_fusion.1
  140.8 3.5 fusion.46
  146.1 2.5 fusion.92
  150.8 2.2 copy.254
  153.1 2.1 reshape.668
  155.1 2.0 copy.215
  157.2 2.1 copy.255
  159.3 3.1 fusion.95
  162.3 2.0 convolution_bitcast_fusion.6
  164.4 11.9 %while.34 = (s32[]{:T(128)}, f32[1,4,64,128]{3,2,1,0:T(8,128)S(1)}, f32[4,1,4,64,128]{4,3,2,1,0:T(8,128)S(1)}, f32[4,1,4,1,1]{2,4,3,1,0:T(1,128)}, f32[4,1,4]{2,...) while((s32[]{:T(128)}, f32[1,4,64,128]{3,2,1,0:T(8,128)S(1)}, ...), condition=%wide.region_5.6_spmd.clone, body=%wide.region_4.5_spmd.clone.sunk | while | flops 131075 | bytes 656552 | solution.py:49
  176.3 2.0 convolution_bitcast_fusion.1
  178.3 6.5 fusion.23
  186.7 1.9 multiply_reduce_fusion.13
  188.6 12.0 %psum.154 = f32[1024]{0:T(1024)S(1)} all-reduce(f32[1024]{0:T(1024)S(1)} %get-tuple-element.382), channel_id=1, replica_groups=mesh['dp'=4,'row'=4,'col'=2] {'row','col'}, use_global_device_ids=true, to_apply=%region_7.8 | all-reduce | flops 1024 | bytes 8192 | tf_op jit(solution)/shard_map/psum | solution.py:196
  200.7 2.1 multiply_reduce_fusion.3
  202.8 14.0 %psum.155 = f32[1024]{0:T(1024)S(1)} all-reduce(f32[1024]{0:T(1024)S(1)} %get-tuple-element.312), channel_id=1, replica_groups=mesh['dp'=4,'row'=4,'col'=2] {'row','col'}, use_global_device_ids=true, to_apply=%region_11.12 | all-reduce | flops 1024 | bytes 8192 | tf_op jit(solution)/shard_map/psum | solution.py:221
  216.7 3.2 fusion.35
  221.4 1.9 multiply_reduce_fusion.1
  223.4 2.0 convolution_bitcast_fusion.5
  225.3 2.7 convolution_bitcast_fusion.4
  230.9 11.6 %while.35 = (s32[]{:T(128)}, f32[1,4,64,128]{3,2,1,0:T(8,128)S(1)}, f32[4,1,4,64,128]{4,3,2,1,0:T(8,128)}, f32[4,1,4]{2,1,0:T(1,128)}, f32[4,1,4,64,128]{4,3,2,1...) while((s32[]{:T(128)}, f32[1,4,64,128]{3,2,1,0:T(8,128)S(1)}, ...), condition=%wide.region_14.15_spmd.clone, body=%wide.region_12.14_spmd.clone.sunk | while | flops 196608 | bytes 787172 | solution.py:49
  242.6 2.3 convolution_bitcast_fusion
  245.7 4.7 fusion.22
  250.4 6.7 %fusion.7 = (f32[4,256,4]{1,2,0:T(4,128)S(1)}, f32[4,256,4]{1,2,0:T(4,128)S(1)}, f32[4,256,4]{1,2,0:T(4,128)S(1)}, f32[4,256,256]{2,1,0:T(8,128)S(1)}) fusion(f32[4,256,4]{1,2,0:T(4,128)S(1)} %bitcast.366, f32[4,256,4]{1,2,0:T(4,128)S(1)} %copy-done.46, f32[4,256,256]{2,1,0:T(8,128)S(1)} %copy-done.35, pred[256,256]{1,0:T(8,128)(4,1)S(1)} %copy-done.45, ...), kind=kOutput, calls=%fused_computation.22 | convolution fusion | flops 818663424 | bytes 4341760 | tf_op jit(solution)/shard_map/transpose(jvp(vmap(clsh,cshp->clhp)))/dot_general | solution.py:39
  257.2 1.9 convolution_bitcast_fusion.2
  259.1 1.9 convolution_add_fusion.1
  261.0 2.0 copy.281
  263.1 2.6 fusion.25
  265.8 2.1 copy.235
  268.4 3.0 multiply_reduce_fusion.7
  271.5 2.6 broadcast_multiply_fusion.1
  274.0 1.9 fusion.33
  277.3 20.1 %reduce-window.16 = f32[1,4,4,2,128]{4,3,2,1,0:T(2,128)S(1)} reduce-window(f32[1,4,4,2,128]{4,3,2,1,0:T(2,128)S(1)} %reshape.690, f32[]{:T(128)} %constant.120.clone.1), window={size=1x1x1x1x128 pad=0_0x0_0x0_0x0_0x0_127}, to_apply=%region_19.20 | reduce-window | flops 520192 | bytes 32772 | tf_op jit(solution)/shard_map/reduce-window.2
  297.5 3.5 fusion.28
  301.4 3.3 fusion.55
  307.2 9.0 %all-reduce.29.cloned.1.call-done = f32[1024,256]{0,1:T(8,128)} async-done(((f32[1024,256]{0,1:T(8,128)}), f32[1024,256]{0,1:T(8,128)}) %all-reduce.29.cloned.1.call-update) | async-done | bytes 1048592 | tf_op jit(solution)/shard_map/psum | solution.py:236
  316.2 2.5 fusion.100
  319.9 19.6 %all-gather.8.cloned.1.call-done = bf16[1024,512]{0,1:T(8,128)(2,1)} async-done(((bf16[1024,256]{0,1:T(8,128)(2,1)}), bf16[1024,512]{0,1:T(8,128)(2,1)}) %all-gather.8.cloned.1.call-update) | async-done | bytes 1048592 | tf_op jit(solution)/shard_map/all_gather | solution.py:200
  339.5 3.3 fusion.96
  344.4 30.1 %all-gather.12.cloned.1.call-done = bf16[2,516,1024]{2,1,0:T(8,128)(2,1)} async-done(((bf16[1,516,1024]{2,1,0:T(8,128)(2,1)}), bf16[2,516,1024]{2,1,0:T(8,128)(2,1)}) %all-gather.12.cloned.1.call-update) | async-done | bytes 2113552 | tf_op jit(solution)/shard_map/all_gather | solution.py:238
  374.5 3.4 reshape.705
  377.9 3.2 fusion.98
  381.2 3.3 convolution_add_fusion
  384.5 3.0 fusion.101
  387.5 47.5 %all-reduce.31.cloned.1.call-done = f32[2,512,256]{2,1,0:T(8,128)} async-done(((f32[2,512,256]{2,1,0:T(8,128)}), f32[2,512,256]{2,1,0:T(8,128)}) %all-reduce.31.cloned.1.call-update) | async-done | bytes 1048592 | tf_op jit(solution)/shard_map/psum | solution.py:265
  435.0 1.9 dynamic-slice_bitcast_fusion
  436.9 4.2 fusion.99
  441.1 3.5 reshape.700
  444.5 1.9 fusion.91
  450.7 17.2 %reduce-scatter.7.cloned.1.call-done = f32[256,512]{1,0:T(8,128)} async-done(((f32[1024,512]{1,0:T(8,128)}), f32[256,512]{1,0:T(8,128)}) %reduce-scatter.7.cloned.1.call-update) | async-done | bytes 524304 | tf_op jit(solution)/shard_map/reduce_scatter | solution.py:202
  468.0 1.9 dynamic-slice_add_fusion
  469.9 31.7 %reduce-scatter.11.cloned.1.call-done = f32[256,512]{1,0:T(8,128)} async-done(((f32[1024,512]{1,0:T(8,128)}), f32[256,512]{1,0:T(8,128)}) %reduce-scatter.11.cloned.1.call-update) | async-done | bytes 524304 | tf_op jit(solution)/shard_map/reduce_scatter | solution.py:244
  502.9 24.5 %all-reduce.22 = (f32[4,256]{1,0:T(4,128)S(1)}, f32[2,512]{1,0:T(2,128)S(1)}, f32[4,256]{1,0:T(4,128)S(1)}, f32[256]{0:T(256)S(1)}) all-reduce(f32[4,256]{1,0:T(4,128)S(1)} %broadcast_multiply_fusion.11, f32[2,512]{1,0:T(2,128)S(1)} %broadcast_multiply_fusion.10, ...), channel_id=1, replica_groups=mesh['dp'=4,'row'=4,'col'=2] {'row','col'}, use_global_device_ids=true, to_apply=%region_25.26 | all-reduce | flops 3328 | bytes 26624 | tf_op jit(solution)/shard_map/psum | solution.py:265
  527.5 21.7 %all-reduce.23 = (f32[512]{0:T(512)}, f32[512,8]{0,1:T(8,128)}, f32[4,256]{1,0:T(4,128)}, f32[256]{0:T(256)}, f32[4,256]{1,0:T(4,128)}, /*index=5*/f32[256]{0:T(...) all-reduce(f32[512]{0:T(512)S(1)} %bitcast.389, ...), channel_id=1, replica_groups=mesh['dp'=4,'row'=4,'col'=2] {'dp'}, use_global_device_ids=true, to_apply=%region_28.29 | all-reduce | flops 7436 | bytes 59488 | tf_op jit(solution)/shard_map/psum | solution.py:281
  549.2 2.0 multiply_add_fusion
  551.2 93.3 %all-reduce.33.cloned.1.call-done = (f32[512,512]{1,0:T(8,128)}, f32[512,512]{1,0:T(8,128)}, f32[512,256]{1,0:T(8,128)}, f32[512,512]{1,0:T(8,128)}) async-done(((f32[512,512]{1,0:T(8,128)}, f32[512,512]{1,0:T(8,128)}, f32[512,256]{1,0:T(8,128)}, f32[512,512]{1,0:T(8,128)}), (f32[512,512]{1,0:T(8,128)}, f32[512,512]{1,0:T(8,128)}, f32[512,256]{1,0:T(8,128)}, ...) | async-done | bytes 3670032 | tf_op jit(solution)/shard_map/psum | solution.py:281
  644.5 2.4 copy.363
  (311 shorter events, 64.7 us)
Async XLA Ops:
  7.2 42.9 %copy-start = (bf16[512,512]{1,0:T(8,128)(2,1)S(1)}, bf16[512,512]{1,0:T(8,128)(2,1)}, u32[]{:S(2)}) copy-start(bf16[512,512]{1,0:T(8,128)(2,1)} %param.35) | copy-start | bytes 1572868
  7.2 3.6 copy-start.77
  7.2 4.5 copy-start.27
  7.2 24.0 %all-gather.6.cloned.1.call-start = ((), (), s32[]{:S(2)}) async-start(), calls=%async_computation.4 | async-start | bytes 1310720 | tf_op jit(solution)/shard_map/all_gather | solution.py:155
  8.7 3.8 copy-start.68
  8.7 3.8 copy-start.39
  9.4 3.4 copy-start.41
  10.8 4.0 copy-start.14
  11.7 38.4 %all-gather.10.cloned.1.call-start = ((), (), s32[]{:S(2)}) async-start(), calls=%async_computation.8 | async-start | bytes 1310720 | tf_op jit(solution)/shard_map/all_gather | solution.py:211
  12.5 117.8 %reduce-scatter.5.cloned.1.call-start = ((), (), s32[]{:S(2)}) async-start(), calls=%async_computation.5 | async-start | bytes 9535488 | tf_op jit(solution)/shard_map/reduce_scatter | solution.py:175
  37.1 163.6 %reduce-scatter.9.cloned.1.call-start = ((), (), s32[]{:S(2)}) async-start(), calls=%async_computation.9 | async-start | bytes 3145728 | tf_op jit(solution)/shard_map/reduce_scatter | solution.py:218
  38.5 139.8 %copy-start.44 = (pred[256,256]{1,0:T(8,128)(4,1)}, pred[256,256]{1,0:T(8,128)(4,1)S(1)}, u32[]{:S(2)}) copy-start(pred[256,256]{1,0:T(8,128)(4,1)S(1)} %iota_compare_fusion) | copy-start | bytes 196612
  38.5 92.7 %copy-start.75 = (f32[4]{0:T(128)}, f32[4]{0:T(128)S(1)}, u32[]{:S(2)}) copy-start(f32[4]{0:T(128)S(1)} %exponential_negate_fusion) | copy-start | bytes 52
  38.5 102.2 %copy-start.52 = (f32[1,256]{1,0:T(1,128)}, f32[1,256]{1,0:T(1,128)S(1)}, u32[]{:S(2)}) copy-start(f32[1,256]{1,0:T(1,128)S(1)} %get-tuple-element.412) | copy-start | bytes 3076
  38.6 102.2 %copy-start.54 = (f32[1,256]{1,0:T(1,128)}, f32[1,256]{1,0:T(1,128)S(1)}, u32[]{:S(2)}) copy-start(f32[1,256]{1,0:T(1,128)S(1)} %get-tuple-element.413) | copy-start | bytes 3076
  38.6 102.2 %copy-start.56 = (f32[1,256]{1,0:T(1,128)}, f32[1,256]{1,0:T(1,128)S(1)}, u32[]{:S(2)}) copy-start(f32[1,256]{1,0:T(1,128)S(1)} %get-tuple-element.414) | copy-start | bytes 3076
  38.6 102.2 %copy-start.58 = (f32[1,256]{1,0:T(1,128)}, f32[1,256]{1,0:T(1,128)S(1)}, u32[]{:S(2)}) copy-start(f32[1,256]{1,0:T(1,128)S(1)} %get-tuple-element.415) | copy-start | bytes 3076
  38.6 102.2 %copy-start.60 = (f32[1,256]{1,0:T(1,128)}, f32[1,256]{1,0:T(1,128)S(1)}, u32[]{:S(2)}) copy-start(f32[1,256]{1,0:T(1,128)S(1)} %get-tuple-element.416) | copy-start | bytes 3076
  38.6 102.2 %copy-start.62 = (f32[1,256]{1,0:T(1,128)}, f32[1,256]{1,0:T(1,128)S(1)}, u32[]{:S(2)}) copy-start(f32[1,256]{1,0:T(1,128)S(1)} %get-tuple-element.417) | copy-start | bytes 3076
  38.6 102.2 %copy-start.64 = (f32[1,256]{1,0:T(1,128)}, f32[1,256]{1,0:T(1,128)S(1)}, u32[]{:S(2)}) copy-start(f32[1,256]{1,0:T(1,128)S(1)} %get-tuple-element.418) | copy-start | bytes 3076
  38.6 102.2 %copy-start.66 = (f32[1,256]{1,0:T(1,128)}, f32[1,256]{1,0:T(1,128)S(1)}, u32[]{:S(2)}) copy-start(f32[1,256]{1,0:T(1,128)S(1)} %get-tuple-element.419) | copy-start | bytes 3076
  38.6 91.7 %copy-start.73 = (f32[4]{0:T(128)S(1)}, f32[4]{0:T(128)}, u32[]{:S(2)}) copy-start(f32[4]{0:T(128)} %param.31) | copy-start | bytes 52
  53.4 262.8 %all-reduce.29.cloned.1.call-start = ((), (), s32[]{:S(2)}) async-start(), calls=%async_computation.10 | async-start | bytes 2097152 | tf_op jit(solution)/shard_map/psum | solution.py:236
  137.2 3.6 copy-start.1
  137.2 3.6 copy-start.78
  137.3 3.6 copy-start.79
  139.7 4.7 copy-start.9
  139.7 4.7 copy-start.11
  146.1 32.3 %copy-start.5 = (f32[4,256,4,64]{1,0,3,2:T(4,128)}, f32[4,256,4,64]{1,0,3,2:T(4,128)S(1)}, u32[]{:S(2)}) copy-start(f32[4,256,4,64]{1,0,3,2:T(4,128)S(1)} %reshape.666) | copy-start | bytes 3145732
  150.8 11.5 %copy-start.16 = (f32[4,256,128]{2,1,0:T(8,128)}, f32[4,256,128]{2,1,0:T(8,128)S(1)}, u32[]{:S(2)}) copy-start(f32[4,256,128]{2,1,0:T(8,128)S(1)} %copy.216) | copy-start | bytes 1572868
  178.3 6.5 copy-start.24
  185.7 15.0 %copy-start.48 = (f32[256]{0:T(256)S(1)}, f32[256]{0:T(256)}, u32[]{:S(2)}) copy-start(f32[256]{0:T(256)} %param.34) | copy-start | bytes 3076
  188.6 28.1 %copy-start.3 = (f32[1024,256]{0,1:T(8,128)}, f32[1024,256]{0,1:T(8,128)S(1)}, u32[]{:S(2)}) copy-start(f32[1024,256]{0,1:T(8,128)S(1)} %get-tuple-element.383) | copy-start | bytes 3145732
  242.6 3.1 copy-start.45
  242.6 3.1 copy-start.46
  250.4 6.8 %copy-start.21 = (f32[4,256,128]{2,1,0:T(8,128)S(1)}, f32[4,256,128]{2,1,0:T(8,128)}, u32[]{:S(2)}) copy-start(f32[4,256,128]{2,1,0:T(8,128)} %copy.215) | copy-start | bytes 1572868
  259.1 3.9 copy-start.18
  263.1 5.0 copy-start.12
  263.1 5.0 copy-start.26
  274.0 23.5 %copy-start.4 = (f32[1024,256]{0,1:T(8,128)S(1)}, f32[1024,256]{0,1:T(8,128)}, u32[]{:S(2)}) copy-start(f32[1024,256]{0,1:T(8,128)} %copy-done.3) | copy-start | bytes 3145732
  274.0 23.5 %copy-start.49 = (f32[256]{0:T(256)S(1)}, f32[256]{0:T(256)}, u32[]{:S(2)}) copy-start(f32[256]{0:T(256)} %param.34) | copy-start | bytes 3076
  275.9 63.5 %all-gather.8.cloned.1.call-start = ((), (), s32[]{:S(2)}) async-start(), calls=%async_computation.6 | async-start | bytes 1572864 | tf_op jit(solution)/shard_map/all_gather | solution.py:200
  301.1 73.4 %all-gather.12.cloned.1.call-start = ((), (), s32[]{:S(2)}) async-start(), calls=%async_computation.13 | async-start | bytes 3194880 | tf_op jit(solution)/shard_map/all_gather | solution.py:238
  301.4 3.3 copy-start.76
  301.4 3.5 copy-start.74
  304.7 11.5 %copy-start.33 = (bf16[1024,512]{1,0:T(8,128)(2,1)S(1)}, bf16[1024,512]{1,0:T(8,128)(2,1)}, u32[]{:S(2)}) copy-start(bf16[1024,512]{1,0:T(8,128)(2,1)} %all-gather.6.cloned.1.call-done) | copy-start | bytes 3145732
  307.1 127.9 %all-reduce.31.cloned.1.call-start = ((), (), s32[]{:S(2)}) async-start(), calls=%async_computation.12 | async-start | bytes 2097152 | tf_op jit(solution)/shard_map/psum | solution.py:265
  319.8 23.3 %copy-start.19 = (bf16[512,512]{0,1:T(8,128)(2,1)S(1)}, bf16[512,512]{0,1:T(8,128)(2,1)}, u32[]{:S(2)}) copy-start(bf16[512,512]{0,1:T(8,128)(2,1)} %copy.282) | copy-start | bytes 1572868
  319.8 23.3 %copy-start.20 = (bf16[512,512]{0,1:T(8,128)(2,1)S(1)}, bf16[512,512]{0,1:T(8,128)(2,1)}, u32[]{:S(2)}) copy-start(bf16[512,512]{0,1:T(8,128)(2,1)} %copy.283) | copy-start | bytes 1572868
  319.9 148.1 %reduce-scatter.7.cloned.1.call-start = ((), (), s32[]{:S(2)}) async-start(), calls=%async_computation.7 | async-start | bytes 2621440 | tf_op jit(solution)/shard_map/reduce_scatter | solution.py:202
  342.8 158.7 %reduce-scatter.11.cloned.1.call-start = ((), (), s32[]{:S(2)}) async-start(), calls=%async_computation.11 | async-start | bytes 2621440 | tf_op jit(solution)/shard_map/reduce_scatter | solution.py:244
  344.4 33.4 %copy-start.31 = (bf16[512,1032]{0,1:T(8,128)(2,1)S(1)}, bf16[512,1032]{0,1:T(8,128)(2,1)}, u32[]{:S(2)}) copy-start(bf16[512,1032]{0,1:T(8,128)(2,1)} %reshape.696) | copy-start | bytes 3170308
  377.9 3.3 copy-start.25
  377.9 3.3 copy-start.40
  381.1 3.3 copy-start.32
  384.4 260.0 %all-reduce.33.cloned.1.call-start = ((), (), s32[]{:S(2)}) async-start(), calls=%async_computation.14 | async-start | bytes 7340032 | tf_op jit(solution)/shard_map/psum | solution.py:281
  384.5 52.4 %copy-start.34 = (bf16[1024,512]{1,0:T(8,128)(2,1)S(1)}, bf16[1024,512]{1,0:T(8,128)(2,1)}, u32[]{:S(2)}) copy-start(bf16[1024,512]{1,0:T(8,128)(2,1)} %all-gather.6.cloned.1.call-done) | copy-start | bytes 3145732
  449.0 18.9 %copy-start.13 = (f32[256,1024]{1,0:T(8,128)S(1)}, f32[256,1024]{1,0:T(8,128)}, u32[]{:S(2)}) copy-start(f32[256,1024]{1,0:T(8,128)} %param.20) | copy-start | bytes 3145732
  449.0 52.5 %copy-start.15 = (f32[256,1024]{1,0:T(8,128)S(1)}, f32[256,1024]{1,0:T(8,128)}, u32[]{:S(2)}) copy-start(f32[256,1024]{1,0:T(8,128)} %copy-done.14) | copy-start | bytes 3145732
  449.1 78.4 %copy-start.69 = (f32[256]{0:T(256)S(1)}, f32[256]{0:T(256)}, u32[]{:S(2)}) copy-start(f32[256]{0:T(256)} %get-tuple-element.311) | copy-start | bytes 3076
  449.1 100.1 %copy-start.28 = (f32[256,512]{1,0:T(8,128)S(1)}, f32[256,512]{1,0:T(8,128)}, u32[]{:S(2)}) copy-start(f32[256,512]{1,0:T(8,128)} %param.21) | copy-start | bytes 1572868
  449.1 100.1 %copy-start.51 = (f32[256]{0:T(256)S(1)}, f32[256]{0:T(256)}, u32[]{:S(2)}) copy-start(f32[256]{0:T(256)} %copy-done.50) | copy-start | bytes 3076
  644.5 3.4 copy-start.43
  644.5 4.2 copy-start.36
  (30 other events, 66.8 us)
Sparse Core Ops, SparseCore 0:
  11.8 19.4 all-gather.5
  33.4 16.6 all-gather.9
  52.4 77.8 reduce-scatter.4
  132.4 31.9 reduce-scatter.8
  276.1 40.0 all-reduce.28
  318.2 21.2 all-gather.7
  341.0 33.4 all-gather.11
  378.2 56.6 all-reduce.30
  437.5 30.4 reduce-scatter.6
  470.3 31.1 reduce-scatter.10
  505.3 139.0 all-reduce.32
where the time goes:
time: 666 us; the launch traced here: 657 us
  waiting for transfers between devices  349 us (52%)
  other arithmetic  80 us (12%)
  blocking collectives  72.2 us (11%)
  local copies, waits for them, and re-layouts  71.6 us (11%)
  matrix products  67.1 us (10%)
  between operations  15.6 us (2%)
    psum x1, waiting for transfers between devices, body(): lax.psum((gain_mine, grad_weight_z, grad_weight_x, grad_weight_dt, bc_min...  93.3 us
    reduce_scatter x1, waiting for transfers between devices, body(): lax.psum_scatter(partial_proj, 'col', scatter_dimension=1, tiled=True)  76.8 us
    psum x1, waiting for transfers between devices, body(): lax.psum((row_hot[:, None] * input_dot[None, :], col_hot[:, None] * gain_...  47.5 us
    reduce_scatter x1, waiting for transfers between devices, body(): lax.psum_scatter(heads_term + jnp.dot(bc_total, bc_wide.T, precision=PREC...  31.7 us
    all_gather x1, waiting for transfers between devices, body(): grad_cols = lax.all_gather(grad_slot, 'col', axis=1, tiled=True)  30.1 us
    another operation x9, other arithmetic  28.7 us
    psum x1, blocking collectives, body(): lax.psum((row_hot[:, None] * input_dot[None, :], col_hot[:, None] * gain_...  24.5 us
    psum x1, blocking collectives, body(): lax.psum((gain_mine, grad_weight_z, grad_weight_x, grad_weight_dt, bc_min...  21.7 us
  transfers between devices with their start and end apart: 11, of which 10 were waited for; matrix products, arithmetic and copies ran while one was open for 22% of the time, Pallas kernels for 0%

commit v1 on v0

v1 whole, which is shorter than its diff:
```python
import functools

import jax
import jax.numpy as jnp
from jax import lax
from jax.experimental import pallas as pl
from jax.experimental.pallas import tpu as pltpu
from jax.sharding import PartitionSpec as P

BLOCK = 256
SEQ_LEN = 1024
LANES = 128
HALO = 8
EPSILON = 1e-05
PRECISE = lax.Precision.HIGHEST
F32 = jnp.float32
BF16 = jnp.bfloat16


def dot_f32(a, b):
    return jnp.dot(a, b, precision=PRECISE, preferred_element_type=F32)


def dot_nn(a, b):
    return lax.dot_general(a, b, (((1,), (0,)), ((), ())), preferred_element_type=F32)


def dot_nt(a, b):
    return lax.dot_general(a, b, (((1,), (1,)), ((), ())), preferred_element_type=F32)


def dot_tn(a, b):
    return lax.dot_general(a, b, (((0,), (0,)), ((), ())), preferred_element_type=F32)


def sigmoid(v):
    return 1.0 / (1.0 + jnp.exp(-v))


def iota(shape, axis):
    return lax.broadcasted_iota(jnp.int32, shape, axis)


def head_spread(chan, head_width):
    head = iota((LANES, chan), 0)
    lane = iota((LANES, chan), 1)
    return ((lane >= head * head_width) & (lane < (head + 1) * head_width)).astype(F32)


def block_terms(ext_ref, step_raw, conv_ref, head_ref, chan, head_width):
    rows = step_raw.shape[0]
    pre = conv_ref[4:5, :]
    for tap in range(4):
        first = HALO - 3 + tap
        pre = pre + conv_ref[tap : tap + 1, :] * ext_ref[first : first + rows, :]
    gate = sigmoid(pre)
    conv = pre * gate
    step_pre = step_raw + head_ref[0:1, :]
    step = jnp.maximum(step_pre, 0.0) + jnp.log1p(jnp.exp(-jnp.abs(step_pre)))
    rate = -jnp.exp(head_ref[1:2, :])
    causal = iota((rows, rows), 0) >= iota((rows, rows), 1)
    log_decay = dot_f32(causal.astype(F32), step * rate)
    spread = head_spread(chan, head_width)
    step_ch = dot_f32(step, spread)
    log_ch = dot_f32(log_decay, spread)
    skip_ch = dot_f32(jnp.broadcast_to(head_ref[2:3, :], (HALO, LANES)), spread)[0:1, :]
    return pre, gate, conv, step_pre, step, rate, causal, log_decay, spread, step_ch, log_ch, skip_ch


def forward_kernel(heads, head_width, proj_ref, conv_ref, head_ref, gated_ref, mixed_ref, inside_ref, state_ref, ext, state):
    chan = heads * head_width
    rows = proj_ref.shape[0]
    wide = ext.shape[1]

    @pl.when(pl.program_id(0) == 0)
    def _():
        ext[...] = jnp.zeros_like(ext)
        state[...] = jnp.zeros_like(state)

    ext[0:HALO, :] = ext[rows : rows + HALO, :]
    ext[HALO : HALO + rows, :] = proj_ref[:, chan : chan + wide]
    z_raw = proj_ref[:, 0:chan]
    terms = block_terms(ext, proj_ref[:, chan + wide :], conv_ref, head_ref, chan, head_width)
    _, _, conv, _, step, _, causal, log_decay, _, step_ch, log_ch, skip_ch = terms
    half = (wide - chan) // 2
    x_conv = conv[:, :chan]
    b_half = conv[:, chan : chan + half].astype(BF16)
    c_half = conv[:, chan + half :].astype(BF16)
    stepped = x_conv * step_ch
    stepped_half = stepped.astype(BF16)
    scores = dot_nt(c_half, b_half)
    log_rows = log_decay.T
    lane = iota((rows, chan), 1)
    inside = jnp.zeros((rows, chan), F32)
    for head in range(heads):
        gap = log_decay[:, head : head + 1] - log_rows[head : head + 1, :]
        mixing = (scores * jnp.exp(jnp.where(causal, gap, -1e30))).astype(BF16)
        mine = (lane >= head * head_width) & (lane < (head + 1) * head_width)
        inside = inside + dot_nn(mixing, jnp.where(mine, stepped, 0.0).astype(BF16))
    entering = state[...]
    state_ref[0] = entering
    outside = dot_nn(c_half, entering.astype(BF16)) * jnp.exp(log_ch)
    mixed = inside + outside + skip_ch * x_conv
    last = log_ch[rows - 1 : rows, :]
    tail = stepped * jnp.exp(last - log_ch)
    state[...] = entering * jnp.exp(last) + dot_tn(b_half, tail.astype(BF16))
    gated_ref[...] = mixed * (z_raw * sigmoid(z_raw))
    mixed_ref[...] = mixed
    inside_ref[...] = inside


def backward_kernel(
    heads, head_width, proj_ref, prior_ref, conv_ref, head_ref, mixed_ref, inside_ref, state_ref, grad_ref,
    slot_ref, conv_grad_ref, head_grad_ref, skip_grad_ref, ext, grad_ext, grad_state,
):
    chan = heads * head_width
    rows = proj_ref.shape[0]
    wide = ext.shape[1]
    turn = pl.program_id(0)
    first_block = turn == pl.num_programs(0) - 1

    @pl.when(turn == 0)
    def _():
        grad_ext[...] = jnp.zeros_like(grad_ext)
        grad_state[...] = jnp.zeros_like(grad_state)
        conv_grad_ref[...] = jnp.zeros_like(conv_grad_ref)
        head_grad_ref[...] = jnp.zeros_like(head_grad_ref)
        skip_grad_ref[...] = jnp.zeros_like(skip_grad_ref)

    ext[0:HALO, :] = jnp.where(first_block, 0.0, prior_ref[:, chan : chan + wide])
    ext[HALO : HALO + rows, :] = proj_ref[:, chan : chan + wide]
    terms = block_terms(ext, proj_ref[:, chan + wide :], conv_ref, head_ref, chan, head_width)
    pre, gate, conv, step_pre, step, rate, causal, log_decay, spread, step_ch, log_ch, skip_ch = terms
    half = (wide - chan) // 2
    x_conv = conv[:, :chan]
    b_half = conv[:, chan : chan + half].astype(BF16)
    c_half = conv[:, chan + half :].astype(BF16)
    stepped = x_conv * step_ch
    stepped_half = stepped.astype(BF16)
    grad_mixed = grad_ref[...]
    grad_half = grad_mixed.astype(BF16)
    inside = inside_ref[...]
    outside = mixed_ref[...] - inside - skip_ch * x_conv

    scores = dot_nt(c_half, b_half)
    log_rows = log_decay.T
    lane = iota((rows, chan), 1)
    grad_scores = jnp.zeros((rows, rows), F32)
    grad_inner = jnp.zeros((rows, chan), F32)
    for head in range(heads):
        gap = log_decay[:, head : head + 1] - log_rows[head : head + 1, :]
        decay = jnp.exp(jnp.where(causal, gap, -1e30))
        mixing = (scores * decay).astype(BF16)
        mine = (lane >= head * head_width) & (lane < (head + 1) * head_width)
        grad_mine = jnp.where(mine, grad_mixed, 0.0).astype(BF16)
        grad_scores = grad_scores + dot_nt(grad_mine, stepped_half) * decay
        grad_inner = grad_inner + dot_tn(mixing, grad_mine)
    scores_half = grad_scores.astype(BF16)

    entering = state_ref[0]
    left = grad_state[...]
    left_half = left.astype(BF16)
    grad_outer = (grad_mixed * jnp.exp(log_ch)).astype(BF16)
    last = log_ch[rows - 1 : rows, :]
    fade = jnp.exp(last - log_ch)
    tail = stepped * fade
    grad_tail = dot_nn(b_half, left_half)
    tail_term = tail * grad_tail
    grad_c = dot_nt(grad_outer, entering.astype(BF16)) + dot_nn(scores_half, b_half)
    grad_b = dot_nt(tail.astype(BF16), left_half) + dot_tn(scores_half, c_half)
    grad_last = jnp.sum(tail_term, axis=0, keepdims=True) + jnp.exp(last) * jnp.sum(
        left * entering, axis=0, keepdims=True
    )
    grad_state[...] = left * jnp.exp(last) + dot_tn(c_half, grad_outer)

    grad_stepped = grad_inner + grad_tail * fade
    log_term = (
        grad_half.astype(F32) * inside
        + grad_mixed * outside
        - stepped_half.astype(F32) * grad_inner
        - tail_term
    )
    row = iota((rows, chan), 0)
    log_term = log_term + jnp.where(row == rows - 1, grad_last, 0.0)

    def per_head(values):
        return lax.dot_general(
            values, spread, (((1,), (1,)), ((), ())), precision=PRECISE, preferred_element_type=F32
        )

    later = (iota((rows, rows), 0) <= iota((rows, rows), 1)).astype(F32)
    grad_rate_step = dot_f32(later, per_head(log_term))
    grad_step = per_head(grad_stepped * x_conv) + grad_rate_step * rate
    grad_step_raw = grad_step * sigmoid(step_pre)
    head_grad_ref[0:1, :] += jnp.sum(grad_step_raw, axis=0, keepdims=True)
    head_grad_ref[1:2, :] += jnp.sum(grad_rate_step * step, axis=0, keepdims=True) * rate
    skip_grad_ref[0:1, :] += jnp.sum(grad_mixed * x_conv, axis=0, keepdims=True)

    grad_x = grad_stepped * step_ch + grad_mixed * skip_ch
    slope = gate * (1.0 + pre * (1.0 - gate))
    grad_ext[rows : rows + HALO, :] = grad_ext[0:HALO, :]
    grad_ext[0:rows, 0:chan] = grad_x * slope[:, :chan]
    grad_ext[0:rows, chan : chan + half] = grad_b * slope[:, chan : chan + half]
    grad_ext[0:rows, chan + half :] = grad_c * slope[:, chan + half :]
    grad_pre = grad_ext[0:rows, :]
    grad_raw = jnp.zeros((rows, wide), F32)
    for tap in range(4):
        grad_raw = grad_raw + conv_ref[tap : tap + 1, :] * grad_ext[3 - tap : 3 - tap + rows, :]
        first = HALO - 3 + tap
        conv_grad_ref[tap : tap + 1, :] += jnp.sum(
            grad_pre * ext[first : first + rows, :], axis=0, keepdims=True
        )
    conv_grad_ref[4:5, :] += jnp.sum(grad_pre, axis=0, keepdims=True)
    slot_ref[:, 0:wide] = grad_raw.astype(BF16)
    slot_ref[:, wide:] = grad_step_raw.astype(BF16)


def mixer_forward(proj, conv_pack, head_pack, heads, head_width, wide):
    total, columns = proj.shape
    chan = heads * head_width
    state_width = (wide - chan) // 2
    blocks = total // BLOCK
    row_spec = pl.BlockSpec((BLOCK, chan), lambda i: (i, 0))
    rows = jax.ShapeDtypeStruct((total, chan), F32)
    return pl.pallas_call(
        functools.partial(forward_kernel, heads, head_width),
        grid=(blocks,),
        in_specs=[
            pl.BlockSpec((BLOCK, columns), lambda i: (i, 0)),
            pl.BlockSpec(conv_pack.shape, lambda i: (0, 0)),
            pl.BlockSpec(head_pack.shape, lambda i: (0, 0)),
        ],
        out_specs=[row_spec, row_spec, row_spec, pl.BlockSpec((1, state_width, chan), lambda i: (i, 0, 0))],
        out_shape=[rows, rows, rows, jax.ShapeDtypeStruct((blocks, state_width, chan), F32)],
        scratch_shapes=[pltpu.VMEM((BLOCK + HALO, wide), F32), pltpu.VMEM((state_width, chan), F32)],
        compiler_params=pltpu.CompilerParams(vmem_limit_bytes=32 << 20),
        cost_estimate=pl.CostEstimate(flops=4 * 10**9, bytes_accessed=7 << 20, transcendentals=2 << 20),
        name="mixer_forward",
    )(proj, conv_pack, head_pack)


def mixer_backward(proj, conv_pack, head_pack, mixed, inside, states, grad_mixed, heads, head_width, wide):
    total, columns = proj.shape
    chan = heads * head_width
    state_width = (wide - chan) // 2
    blocks = total // BLOCK
    ratio = BLOCK // HALO
    back = lambda i: (blocks - 1 - i, 0)
    row_spec = pl.BlockSpec((BLOCK, chan), back)
    fixed = lambda i: (0, 0)
    out_columns = wide + LANES
    return pl.pallas_call(
        functools.partial(backward_kernel, heads, head_width),
        grid=(blocks,),
        in_specs=[
            pl.BlockSpec((BLOCK, columns), back),
            pl.BlockSpec((HALO, columns), lambda i: (jnp.maximum((blocks - 1 - i) * ratio - 1, 0), 0)),
            pl.BlockSpec(conv_pack.shape, fixed),
            pl.BlockSpec(head_pack.shape, fixed),
            row_spec,
            row_spec,
            pl.BlockSpec((1, state_width, chan), lambda i: (blocks - 1 - i, 0, 0)),
            row_spec,
        ],
        out_specs=[
            pl.BlockSpec((BLOCK, out_columns), back),
            pl.BlockSpec((HALO, wide), fixed),
            pl.BlockSpec((HALO, LANES), fixed),
            pl.BlockSpec((HALO, chan), fixed),
        ],
        out_shape=[
            jax.ShapeDtypeStruct((total, out_columns), BF16),
            jax.ShapeDtypeStruct((HALO, wide), F32),
            jax.ShapeDtypeStruct((HALO, LANES), F32),
            jax.ShapeDtypeStruct((HALO, chan), F32),
        ],
        scratch_shapes=[
            pltpu.VMEM((BLOCK + HALO, wide), F32),
            pltpu.VMEM((BLOCK + HALO, wide), F32),
            pltpu.VMEM((state_width, chan), F32),
        ],
        compiler_params=pltpu.CompilerParams(vmem_limit_bytes=40 << 20),
        cost_estimate=pl.CostEstimate(flops=12 * 10**9, bytes_accessed=9 << 20, transcendentals=2 << 20),
        name="mixer_backward",
    )(proj, proj, conv_pack, head_pack, mixed, inside, states, grad_mixed)


def from_columns(block_for):
    count = lax.axis_size("col")
    got = [block_for(0)]
    for j in range(1, count):
        pairs = [((i + j) % count, i) for i in range(count)]
        got.append(lax.ppermute(block_for((count - j) % count), "col", pairs))
    return got


def scatter_sum(partial):
    rows, cols = lax.axis_size("row"), lax.axis_size("col")
    pair = 2 if rows % 2 == 0 else 1
    chips = rows // pair
    row = lax.axis_index("row")
    chip, core = row // pair, row % pair
    tokens, width = partial.shape[0] // rows, partial.shape[1] // cols
    blocks = partial.reshape(chips, pair, tokens, cols * width)
    keep = lax.dynamic_index_in_dim(blocks, core, 1, keepdims=False)
    if pair == 2:
        send = lax.dynamic_index_in_dim(blocks, 1 - core, 1, keepdims=False).astype(BF16)
        swap = [(i, i ^ 1) for i in range(rows)]
        keep = keep + lax.ppermute(send, "row", swap).astype(F32)
    total = None
    for dx in range(chips):
        mine = lax.dynamic_index_in_dim(keep, (chip + dx) % chips, 0, keepdims=False)
        for dc in range(cols):
            piece = mine[:, dc * width : (dc + 1) * width]
            if dx or dc:
                pairs = []
                for r in range(rows):
                    for c in range(cols):
                        there = ((r // pair + dx) % chips) * pair + r % pair
                        pairs.append((r * cols + c, there * cols + (c + dc) % cols))
                piece = lax.ppermute(piece.astype(BF16), ("row", "col"), pairs).astype(F32)
            total = piece if total is None else total + piece
    return total


def pad_to(matrix, rows, columns):
    return jnp.pad(matrix, ((0, rows - matrix.shape[0]), (0, columns - matrix.shape[1])))


def body(
    hidden,
    cotangent,
    norm_gain,
    weight_z,
    weight_x,
    weight_dt,
    weight_bc,
    conv_weight,
    conv_bias,
    bc_conv_weight,
    bc_conv_bias,
    dt_bias,
    decay_log,
    skip_gain,
    gate_gain,
    out_weight,
):
    row_count = lax.axis_size("row")
    col_count = lax.axis_size("col")
    col_index = lax.axis_index("col")
    model_width = hidden.shape[1]
    width = weight_z.shape[0]
    chan = weight_z.shape[1] // col_count
    heads = weight_dt.shape[1] // col_count
    head_width = chan // heads
    bc_width = weight_bc.shape[1]
    wide = chan + bc_width
    inner = chan * row_count * col_count

    def own_first(matrix, axis):
        return jnp.roll(matrix, -col_index * width, axis)

    def by_col(matrix, k):
        split = matrix.reshape(matrix.shape[0], col_count, matrix.shape[1] // col_count)
        return lax.dynamic_index_in_dim(split, (col_index + k) % col_count, 1, keepdims=False)

    def weights_for(k):
        return jnp.concatenate(
            [by_col(weight_z, k), by_col(weight_x, k), weight_bc, by_col(weight_dt, k)], axis=1
        )

    weights = jnp.concatenate(from_columns(weights_for), axis=0)
    weights = jnp.pad(weights, ((0, 0), (0, LANES - heads)))

    def out_rows_for(k):
        split = out_weight.reshape(col_count, chan, out_weight.shape[1])
        return lax.dynamic_index_in_dim(split, (col_index + k) % col_count, 0, keepdims=False)

    out_own = jnp.concatenate(from_columns(out_rows_for), axis=1)
    cot_half = cotangent.astype(BF16)
    cot_wide = jnp.concatenate(from_columns(lambda k: cot_half), axis=1)

    inv_rms = lax.rsqrt(jnp.mean(hidden * hidden, axis=1, keepdims=True) + EPSILON)
    scaled = (own_first(hidden, 1) * inv_rms * own_first(norm_gain, 0)[None, :]).astype(BF16)
    gathered = lax.all_gather(scaled, "row", axis=0, tiled=True)
    cot_rows = lax.all_gather(cot_wide, "row", axis=0, tiled=True)
    proj = jnp.dot(gathered, weights, preferred_element_type=F32)

    conv_pack = pad_to(
        jnp.concatenate(
            [
                jnp.concatenate([conv_weight, bc_conv_weight], axis=1),
                jnp.concatenate([conv_bias, bc_conv_bias])[None, :],
            ],
            axis=0,
        ),
        HALO,
        wide,
    )
    head_pack = pad_to(jnp.stack([dt_bias, decay_log, skip_gain]), HALO, LANES)
    gated, mixed, inside, states = mixer_forward(proj, conv_pack, head_pack, heads, head_width, wide)

    grad_gate_out = dot_nt(cot_rows, out_own)
    grad_hat = grad_gate_out * gate_gain[None, :]
    sums = lax.psum(
        jnp.stack([jnp.sum(gated * gated, axis=1), jnp.sum(grad_hat * gated, axis=1)]), ("row", "col")
    )
    inv_gate = lax.rsqrt(sums[0] / inner + EPSILON)[:, None]
    gate_dot = sums[1][:, None] * inv_gate
    gate_hat = gated * inv_gate
    grad_gated = inv_gate * (grad_hat - gate_hat * (gate_dot / inner))
    z_raw = proj[:, :chan]
    z_gate = sigmoid(z_raw)
    grad_mixed = grad_gated * (z_raw * z_gate)
    grad_z = (grad_gated * mixed * (z_gate * (1.0 + z_raw * (1.0 - z_gate)))).astype(BF16)
    gate_out = (gate_hat * gate_gain[None, :]).astype(BF16)
    grad_gate_gain = jnp.sum(grad_gate_out * gate_hat, axis=0)

    slots, conv_grads, head_grads, skip_grads = mixer_backward(
        proj, conv_pack, head_pack, mixed, inside, states, grad_mixed, heads, head_width, wide
    )

    def to_col_blocks(matrix):
        return matrix.reshape(col_count, matrix.shape[0] // col_count, matrix.shape[1])

    def in_col_order(relative, axis):
        return jnp.roll(relative, col_index, axis)

    out_part = dot_tn(gate_out, cot_rows)
    out_rel = from_columns(lambda k: out_part[:, k * width : (k + 1) * width].astype(BF16))
    z_part = dot_tn(gathered, grad_z)
    z_blocks = to_col_blocks(z_part)
    z_rel = from_columns(lambda k: z_blocks[k].astype(BF16))
    early = lax.psum(jnp.concatenate([piece.reshape(-1, chan) for piece in out_rel + z_rel], axis=0), "dp")
    out_size = chan * width // chan
    out_sum = early[: out_size * col_count].reshape(col_count, chan, width)
    z_sum = early[out_size * col_count :].reshape(col_count, width, chan)
    grad_out_weight = in_col_order(out_sum, 0).reshape(col_count * chan, width).astype(F32)
    grad_weight_z = (
        in_col_order(z_sum, 0).transpose(1, 0, 2).reshape(width, col_count * chan).astype(F32)
    )

    branch_out = scatter_sum(dot_nn(gate_out, out_own))
    hidden_col = lax.dynamic_slice_in_dim(hidden, col_index * width, width, 1)
    output = hidden_col + branch_out

    grad_slots = jnp.concatenate([grad_z, slots], axis=1)
    grad_scaled = scatter_sum(dot_nt(grad_slots, weights))

    late_part = dot_tn(gathered, slots)
    weights_f32 = weights.astype(F32)
    gain_part = jnp.sum(z_part * weights_f32[:, :chan], axis=1) + jnp.sum(
        late_part * weights_f32[:, chan:], axis=1
    )
    late_blocks = to_col_blocks(late_part[:, : wide + heads])
    gain_blocks = gain_part.reshape(col_count, 1, width)
    bc_rows = conv_grads[:5, chan:]

    def late_for(k):
        return late_blocks[k].astype(BF16)

    def small_for(k):
        return jnp.concatenate([pad_to(bc_rows, 5, width), gain_blocks[k]], axis=0)

    late_rel = from_columns(late_for)
    small_rel = from_columns(small_for)
    x_rows = [piece[:, :chan] for piece in late_rel]
    dt_rows = [piece[:, wide:].reshape(-1, chan) for piece in late_rel]
    skip_sum = jnp.sum(skip_grads[0].reshape(heads, head_width), axis=1)
    head_row = jnp.concatenate([head_grads[0, :heads], head_grads[1, :heads], skip_sum])[None, :]
    dp_rows = x_rows + dt_rows + [
        conv_grads[:5, :chan].astype(BF16),
        grad_gate_gain[None, :].astype(BF16),
        pad_to(head_row, 1, chan).astype(BF16),
    ]
    late = lax.psum(jnp.concatenate(dp_rows, axis=0), "dp")
    bc_mine = sum(piece[:, chan:wide].astype(F32) for piece in late_rel).astype(BF16)
    small_mine = sum(small_rel)
    shared = lax.psum(
        jnp.concatenate(
            [bc_mine, small_mine[:5, :bc_width].astype(BF16), small_mine[5].reshape(-1, bc_width).astype(BF16)],
            axis=0,
        ),
        ("dp", "row"),
    ).astype(F32)

    dt_count = width * heads // chan
    x_sum = late[: width * col_count].reshape(col_count, width, chan)
    grad_weight_x = (
        in_col_order(x_sum, 0).transpose(1, 0, 2).reshape(width, col_count * chan).astype(F32)
    )
    at = width * col_count
    dt_sum = late[at : at + dt_count * col_count].reshape(col_count, width, heads)
    grad_weight_dt = (
        in_col_order(dt_sum, 0).transpose(1, 0, 2).reshape(width, col_count * heads).astype(F32)
    )
    rest = late[at + dt_count * col_count :].astype(F32)
    grad_weight_bc = shared[:width]
    gain_col = lax.dynamic_slice_in_dim(norm_gain, col_index * width, width, 0)
    grad_norm_gain = shared[width + 5 :].reshape(-1) / gain_col

    normed_col = hidden_col * inv_rms
    grad_in = grad_scaled * gain_col[None, :]
    input_dot = sum(from_columns(lambda k: jnp.sum(grad_in * normed_col, axis=1)))
    grad_hidden = cotangent + inv_rms * (grad_in - normed_col * (input_dot[:, None] / model_width))
    return (
        output,
        grad_hidden,
        grad_norm_gain,
        grad_weight_z,
        grad_weight_x,
        grad_weight_dt,
        grad_weight_bc,
        rest[0:4],
        rest[4],
        shared[width : width + 4],
        shared[width + 4],
        rest[6, :heads],
        rest[6, heads : 2 * heads],
        rest[6, 2 * heads : 3 * heads],
        rest[5],
        grad_out_weight,
    )


def solution(mesh):
    in_specs = (
        P(("dp", "row"), None),
        P(("dp", "row"), "col"),
        P(),
        P("col", "row"),
        P("col", "row"),
        P("col", "row"),
        P("col", None),
        P(None, ("row", "col")),
        P(("row", "col")),
        P(),
        P(),
        P(("row", "col")),
        P(("row", "col")),
        P(("row", "col")),
        P(("row", "col")),
        P("row", "col"),
    )
    out_specs = (
        P(("dp", "row"), "col"),
        P(("dp", "row"), "col"),
        P("col"),
        P("col", "row"),
        P("col", "row"),
        P("col", "row"),
        P("col", None),
        P(None, ("row", "col")),
        P(("row", "col")),
        P(),
        P(),
        P(("row", "col")),
        P(("row", "col")),
        P(("row", "col")),
        P(("row", "col")),
        P("row", "col"),
    )
    return jax.shard_map(body, mesh=mesh, in_specs=in_specs, out_specs=out_specs, check_vma=False)
```

time: 666 us -> 322 us (0.48); the launches traced: 657 us -> 321 us
  waiting for transfers between devices: 349 us -> 170 us
  blocking collectives: 72.2 us -> 14.3 us
  matrix products: 67.1 us -> 13.8 us
  other arithmetic: 80 us -> 32.8 us
  local copies, waits for them, and re-layouts: 71.6 us -> 35.9 us
  Pallas kernels: 0 us -> 21.4 us
  starting transfers between devices: 0.71 us -> 18.2 us
    reduce_scatter x4 -> x0, waiting for transfers between devices: 126 us -> none  [the longest x1 76.8 us: body(): lax.psum_scatter(partial_proj, 'col', scatter_dimension=1, tiled=True)]
    all_gather x4 -> x2, waiting for transfers between devices: 73 us -> 0.01 us  [the longest x1 0.01 us: body(): gathered = lax.all_gather(scaled, 'row', axis=0, tiled=True)]
    psum x4 -> x1, blocking collectives: 72.2 us -> 14.3 us  [body(): lax.psum(jnp.stack([jnp.sum(gated * gated, axis=1), jnp.sum(grad_hat * ga...]
    dot_general x20 -> x7, matrix products: 67.1 us -> 13.8 us  [the longest x2 4.75 us: dot_nt(): lax.dot_general(a, b, (((1,), (1,)), ((), ())), preferred_element_type=F32)]
    ppermute x0 -> x16, waiting for transfers between devices: none -> 43 us  [the longest x8 38.7 us: from_columns(): got.append(lax.ppermute(block_for((count - j) % count), 'col', pairs))]
    another operation x9 -> x4, other arithmetic: 28.7 us -> 0.04 us
    psum x3 -> x2, waiting for transfers between devices: 150 us -> 126 us  [the longest x1 85.2 us: body(): lax.psum(jnp.concatenate([bc_mine, small_mine[:5, :bc_width].astype(BF16)...]
    pallas_call x0 -> x2, Pallas kernels: none -> 21.4 us  [the longest x1 14.6 us: mixer_backward(): pl.pallas_call(functools.partial(backward_kernel, heads, head_width), gri...]
  transfers between devices with their start and end apart: 11 -> 20, of which waited for: 10 -> 9; matrix products, arithmetic and copies ran while one was open for 22% -> 14% of each run, Pallas kernels for 0% -> 2%
where the time goes in v1:
time: 322 us; the launch traced here: 321 us
  waiting for transfers between devices  170 us (53%)
  local copies, waits for them, and re-layouts  35.9 us (11%)
  other arithmetic  32.8 us (10%)
  Pallas kernels  21.4 us (7%)
  starting transfers between devices  18.2 us (6%)
  between operations  14.8 us (5%)
  blocking collectives  14.3 us (4%)
  matrix products  13.8 us (4%)
    psum x1, waiting for transfers between devices, body(): lax.psum(jnp.concatenate([bc_mine, small_mine[:5, :bc_width].astype(BF16)...  85.2 us
    psum x1, waiting for transfers between devices, body(): lax.psum(jnp.concatenate([piece.reshape(-1, chan) for piece in out_rel +...  41.3 us
    ppermute x8, waiting for transfers between devices, from_columns(): got.append(lax.ppermute(block_for((count - j) % count), 'col', pairs))  38.7 us
    pallas_call x1, Pallas kernels, mixer_backward(): pl.pallas_call(functools.partial(backward_kernel, heads, head_width), gri...  14.6 us
    psum x1, blocking collectives, body(): lax.psum(jnp.stack([jnp.sum(gated * gated, axis=1), jnp.sum(grad_hat * ga...  14.3 us
    unnamed x106, local copies, waits for them, and re-layouts  12.1 us
    ppermute x8, starting transfers between devices, from_columns(): got.append(lax.ppermute(block_for((count - j) % count), 'col', pairs))  9.72 us
    ppermute x6, starting transfers between devices, scatter_sum(): piece = lax.ppermute(piece.astype(BF16), ('row', 'col'), pairs).astype(F32)  7.91 us
  transfers between devices with their start and end apart: 20, of which 9 were waited for; matrix products, arithmetic and copies ran while one was open for 14% of the time, Pallas kernels for 2%

profile of v1, /device:TPU:0, one launch (start us, length us, event | category | flops | bytes accessed | tf_op | source)
XLA Modules:
  0.0 320.7 jit_solution(4640869466826886047)
XLA Ops:
  7.3 1.4 multiply_reduce_fusion.3
  8.7 0.8 fusion.41
  9.5 2.3 fusion.19
  11.9 3.1 collective-permute-start.1
  15.0 6.3 %collective-permute-done.1 = bf16[256,512]{1,0:T(8,128)(2,1)S(1)} collective-permute-done((bf16[256,512]{1,0:T(8,128)(2,1)S(1)}, bf16[256,512]{1,0:T(8,128)(2,1)S(1)}, u32[]{:S(2)}, u32[]{:S(2)}) %collective-permute-start.1) | collective-permute-done | bytes 262176 | tf_op jit(solution)/shard_map/ppermute | solution.py:293
  21.3 0.9 pad_maximum_fusion.2
  23.2 1.8 collective-permute-start
  25.0 0.7 dynamic-slice_bitcast_fusion.3
  26.5 17.3 %collective-permute-done = bf16[512,772]{0,1:T(8,128)(2,1)S(1)} collective-permute-done((bf16[512,772]{0,1:T(8,128)(2,1)S(1)}, bf16[512,772]{0,1:T(8,128)(2,1)S(1)}, u32[]{:S(2)}, u32[]{:S(2)}) %collective-permute-start) | collective-permute-done | bytes 790560 | tf_op jit(solution)/shard_map/ppermute | solution.py:293
  43.9 6.5 %fusion.50 = f32[1024,896]{0,1:T(8,128)} fusion(bf16[512,772]{0,1:T(8,128)(2,1)S(1)} %collective-permute-done, bf16[512,4]{0,1:T(4,128)(2,1)S(1)} %get-tuple-element.133, bf16[512,256]{0,1:T(8,128)(2,1)S(1)} %copy.121, bf16[512,256]{0,1:T(8,128)(2,1)S(1)} %get-tuple-element.127, bf16[512,256]{0,1:T(8,128)(2,1)S(1)} %get-tuple-element.143), kind=kLoop, calls=%fused_computation.133 | loop fusion | flops 14680064 | bytes 5251072 | tf_op jit(solution)/shard_map/convert_element_type | solution.py:451
  50.3 3.9 %fusion.48.proj_ref.prior_ref = f32[1024,896]{1,0:T(8,128)S(1)} fusion(bf16[1024,1024]{1,0:T(8,128)(2,1)} %all-gather.3.cloned.1.call-done, bf16[512,772]{0,1:T(8,128)(2,1)S(1)} %collective-permute-done, bf16[512,4]{0,1:T(4,128)(2,1)S(1)} %get-tuple-element.133, bf16[512,256]{0,1:T(8,128)(2,1)S(1)} %copy.121, bf16[512,256]{0,1:T(8,128)(2,1)S(1)} %get-tuple-element.127, ...), kind=kOutput, calls=%fused_computation.132 | convolution fusion | flops 1893728256 | bytes 7348224 | tf_op jit(solution)/shard_map/dot_general | solution.py:387
  54.3 6.8 %mixer_forward.1 = (f32[1024,256]{1,0:T(8,128)S(1)}, f32[1024,256]{1,0:T(8,128)S(1)}, f32[1024,256]{1,0:T(8,128)S(1)}, f32[4,128,256]{2,1,0:T(8,128)S(1)}) custom-call(f32[1024,896]{1,0:T(8,128)S(1)} %fusion.48.proj_ref.prior_ref, f32[8,512]{1,0:T(8,128)S(1)} %select_maximum_fusion.conv_ref, f32[8,128]{1,0:T(8,128)S(1)} %select_maximum_fusion.2.head_ref), custom_call_target="tpu_custom_call" | custom-call | flops 4000000000 | bytes 7340032 | tf_op jit(solution)/shard_map/mixer_forward/pallas_call | solution.py:225
  61.2 1.0 copy-done.2
  62.1 0.8 copy-done.4
  63.6 2.4 multiply_reduce_fusion.2
  66.1 14.3 %psum.28 = f32[2,1024]{1,0:T(2,128)S(1)} all-reduce(f32[2,1024]{1,0:T(2,128)S(1)} %pad_maximum_fusion.7), channel_id=1, replica_groups=mesh['dp'=4,'row'=4,'col'=2] {'row','col'}, use_global_device_ids=true, to_apply=%region_3.4 | all-reduce | flops 2048 | bytes 16384 | tf_op jit(solution)/shard_map/psum | solution.py:405
  80.4 2.1 multiply_convert_fusion
  83.2 14.6 %mixer_backward.1 = (bf16[1024,640]{1,0:T(8,128)(2,1)S(1)}, f32[8,512]{1,0:T(8,128)S(1)}, f32[8,128]{1,0:T(8,128)S(1)}, f32[8,256]{1,0:T(8,128)S(1)}) custom-call(f32[1024,896]{1,0:T(8,128)S(1)} %copy-done.1, f32[1024,896]{1,0:T(8,128)S(1)} %copy-done.1, f32[8,512]{1,0:T(8,128)S(1)} %select_maximum_fusion.conv_ref, ...), custom_call_target="tpu_custom_call" | custom-call | flops 12000000000 | bytes 9437184 | tf_op jit(solution)/shard_map/mixer_backward/pallas_call | solution.py:252
  97.8 1.6 fusion.52
  99.4 0.9 slice.234
  101.0 1.9 fusion.60
  102.9 1.6 copy.132
  104.5 1.5 fusion.20
  106.5 1.6 collective-permute-start.12
  108.2 2.3 fusion.10
  110.8 0.8 copy-done.17
  111.9 0.8 fusion.32
  114.3 1.6 copy-done.14
  115.9 0.9 convolution_convert_fusion
  119.7 12.2 %collective-permute-done.14 = bf16[256,512]{1,0:T(8,128)(2,1)S(1)} collective-permute-done((bf16[256,512]{1,0:T(8,128)(2,1)S(1)}, bf16[256,512]{1,0:T(8,128)(2,1)S(1)}, u32[]{:S(2)}, u32[]{:S(2)}) %collective-permute-start.14) | collective-permute-done | bytes 262176 | tf_op jit(solution)/shard_map/ppermute | solution.py:293
  132.0 1.1 add_convert_fusion
  133.1 0.8 pad_maximum_fusion.6
  134.2 2.0 pad_maximum_fusion
  137.4 1.0 slice.247
  138.4 1.0 concatenate.81
  139.4 85.2 %all-reduce.9.cloned.1.call-done = bf16[519,256]{0,1:T(8,128)(2,1)} async-done(((bf16[519,256]{0,1:T(8,128)(2,1)}), bf16[519,256]{0,1:T(8,128)(2,1)}) %all-reduce.9.cloned.1.call-update) | async-done | bytes 265744 | tf_op jit(solution)/shard_map/psum | solution.py:479
  224.7 0.9 slice.240
  225.7 1.0 convert_element_type.164
  227.4 2.2 bitcast_add_fusion
  229.8 1.9 collective-permute-start.10
  231.6 1.1 collective-permute-start.9
  233.5 1.8 bitcast_add_fusion.1
  235.4 0.8 fusion.57
  236.2 1.7 collective-permute-start.6
  237.9 1.1 collective-permute-start.5
  239.9 1.5 collective-permute-start.4
  241.4 4.2 %collective-permute-done.9 = bf16[256,512]{1,0:T(8,128)(2,1)S(1)} collective-permute-done((bf16[256,512]{1,0:T(8,128)(2,1)S(1)}, bf16[256,512]{1,0:T(8,128)(2,1)S(1)}, u32[]{:S(2)}, u32[]{:S(2)}) %collective-permute-start.9) | collective-permute-done | bytes 262176 | tf_op jit(solution)/shard_map/ppermute | solution.py:321
  246.3 1.2 collective-permute-start.11
  247.5 0.7 slice_reduce_fusion.1
  248.2 0.9 slice.253
  249.1 2.0 copy.149
  251.8 1.6 copy.151
  253.3 2.8 collective-permute-done.11
  256.3 2.8 multiply_add_fusion
  259.1 41.3 %all-reduce.11.cloned.1.call-done = (bf16[2048,256]{1,0:T(8,128)(2,1)}, bf16[1047,256]{0,1:T(8,128)(2,1)}) async-done(((bf16[2048,256]{1,0:T(8,128)(2,1)}, bf16[1047,256]{0,1:T(8,128)(2,1)}), (bf16[2048,256]{1,0:T(8,128)(2,1)}, bf16[1047,256]{0,1:T(8,128)(2,1)})) %all-reduce.11.cloned.1.call-update) | async-done | bytes 1584656 | tf_op jit(solution)/shard_map/psum | solution.py:434
  300.3 1.2 slice.251
  301.5 0.8 slice.252
  302.3 0.9 slice_convert_fusion.2
  303.3 0.8 slice_reduce_fusion
  305.1 1.1 copy.158
  306.6 1.8 convert_bitcast_fusion
  308.4 1.0 copy.145
  309.4 1.0 copy.160
  313.0 1.1 bitcast_convert_fusion.2
  (200 shorter events, 18.9 us)
Async XLA Ops:
  7.2 4.7 %copy-start.15 = (f32[256,512]{1,0:T(8,128)S(1)}, f32[256,512]{1,0:T(8,128)}, u32[]{:S(2)}) copy-start(f32[256,512]{1,0:T(8,128)} %param.19) | copy-start | bytes 1572868
  7.2 43.1 %all-gather.3.cloned.1.call-start = ((), (), s32[]{:S(2)}) async-start(), calls=%async_computation | async-start | bytes 2621440 | tf_op jit(solution)/shard_map/all_gather | solution.py:385
  9.5 12.8 %copy-start.41 = (bf16[512,8]{0,1:T(8,128)(2,1)S(1)}, bf16[512,8]{0,1:T(8,128)(2,1)}, u32[]{:S(2)}) copy-start(bf16[512,8]{0,1:T(8,128)(2,1)} %param.23) | copy-start | bytes 24580
  9.5 12.8 %copy-start.38 = (bf16[512,256]{1,0:T(8,128)(2,1)S(1)}, bf16[512,256]{1,0:T(8,128)(2,1)}, u32[]{:S(2)}) copy-start(bf16[512,256]{1,0:T(8,128)(2,1)} %param.24) | copy-start | bytes 786436
  11.7 10.7 %copy-start.33 = (bf16[512,512]{1,0:T(8,128)(2,1)S(1)}, bf16[512,512]{1,0:T(8,128)(2,1)}, u32[]{:S(2)}) copy-start(bf16[512,512]{1,0:T(8,128)(2,1)} %param.22) | copy-start | bytes 1572868
  11.8 10.9 %copy-start.34 = (bf16[512,512]{1,0:T(8,128)(2,1)S(1)}, bf16[512,512]{1,0:T(8,128)(2,1)}, u32[]{:S(2)}) copy-start(bf16[512,512]{1,0:T(8,128)(2,1)} %param.21) | copy-start | bytes 1572868
  11.8 51.2 %all-gather.5.cloned.1.call-start = ((), (), s32[]{:S(2)}) async-start(), calls=%async_computation.1 | async-start | bytes 2621440 | tf_op jit(solution)/shard_map/all_gather | solution.py:386
  11.9 9.4 %collective-permute-start.1 = (bf16[256,512]{1,0:T(8,128)(2,1)S(1)}, bf16[256,512]{1,0:T(8,128)(2,1)S(1)}, u32[]{:S(2)}, u32[]{:S(2)}) collective-permute-start(bf16[256,512]{1,0:T(8,128)(2,1)S(1)} %convert_element_type.144), channel_id=1, source_target_pairs={{1,0},{0,1},{3,2},{2,3},{5,4},{4,5},{7,6},{6,7},{9,8},{8,9},{11,10... | collective-permute-start | bytes 786440 | tf_op jit(solution)/shard_map/ppermute | solution.py:293
  22.2 202.5 %all-reduce.9.cloned.1.call-start = ((), (), s32[]{:S(2)}) async-start(), calls=%async_computation.2 | async-start | bytes 655360 | tf_op jit(solution)/shard_map/psum | solution.py:479
  22.5 27.9 %copy-start.12 = (bf16[512,256]{0,1:T(8,128)(2,1)}, bf16[512,256]{0,1:T(8,128)(2,1)S(1)}, u32[]{:S(2)}) copy-start(bf16[512,256]{0,1:T(8,128)(2,1)S(1)} %copy.121) | copy-start | bytes 786436
  22.9 2.1 copy-start.32
  22.9 3.5 %copy-start.44 = (f32[256]{0:T(256)S(1)}, f32[256]{0:T(256)}, u32[]{:S(2)}) copy-start(f32[256]{0:T(256)} %param.28) | copy-start | bytes 3076
  23.0 3.5 %copy-start.45 = (f32[256]{0:T(256)S(1)}, f32[256]{0:T(256)}, u32[]{:S(2)}) copy-start(f32[256]{0:T(256)} %param.26) | copy-start | bytes 3076
  23.0 3.5 %copy-start.46 = (f32[4]{0:T(128)S(1)}, f32[4]{0:T(128)}, u32[]{:S(2)}) copy-start(f32[4]{0:T(128)} %param.31) | copy-start | bytes 52
  23.0 3.5 %copy-start.47 = (f32[4]{0:T(128)S(1)}, f32[4]{0:T(128)}, u32[]{:S(2)}) copy-start(f32[4]{0:T(128)} %param.30) | copy-start | bytes 52
  23.0 3.5 %copy-start.48 = (f32[4]{0:T(128)S(1)}, f32[4]{0:T(128)}, u32[]{:S(2)}) copy-start(f32[4]{0:T(128)} %param.29) | copy-start | bytes 52
  23.0 3.5 %copy-start.42 = (f32[4,256]{1,0:T(4,128)S(1)}, f32[4,256]{1,0:T(4,128)}, u32[]{:S(2)}) copy-start(f32[4,256]{1,0:T(4,128)} %param.27) | copy-start | bytes 12292
  23.0 3.5 %copy-start.43 = (f32[4,256]{1,0:T(4,128)S(1)}, f32[4,256]{1,0:T(4,128)}, u32[]{:S(2)}) copy-start(f32[4,256]{1,0:T(4,128)} %param.25) | copy-start | bytes 12292
  23.1 27.2 %copy-start.23 = (bf16[512,256]{0,1:T(8,128)(2,1)}, bf16[512,256]{0,1:T(8,128)(2,1)S(1)}, u32[]{:S(2)}) copy-start(bf16[512,256]{0,1:T(8,128)(2,1)S(1)} %get-tuple-element.127) | copy-start | bytes 786436
  23.1 27.2 %copy-start.25 = (bf16[512,256]{0,1:T(8,128)(2,1)}, bf16[512,256]{0,1:T(8,128)(2,1)S(1)}, u32[]{:S(2)}) copy-start(bf16[512,256]{0,1:T(8,128)(2,1)S(1)} %get-tuple-element.143) | copy-start | bytes 786436
  23.2 20.7 %collective-permute-start = (bf16[512,772]{0,1:T(8,128)(2,1)S(1)}, bf16[512,772]{0,1:T(8,128)(2,1)S(1)}, u32[]{:S(2)}, u32[]{:S(2)}) collective-permute-start(bf16[512,772]{0,1:T(8,128)(2,1)S(1)} %pad_maximum_fusion.1), channel_id=1, source_target_pairs={{1,0},{0,1},{3,2},{2,3},{5,4},{4,5},{7,6},{6,7},{9,8},{8,9},{11,10... | collective-permute-start | bytes 2371592 | tf_op jit(solution)/shard_map/ppermute | solution.py:293
  25.7 37.9 %copy-start.16 = (bf16[256,512]{1,0:T(8,128)(2,1)}, bf16[256,512]{1,0:T(8,128)(2,1)S(1)}, u32[]{:S(2)}) copy-start(bf16[256,512]{1,0:T(8,128)(2,1)S(1)} %get-tuple-element.129) | copy-start | bytes 786436
  25.7 37.2 %collective-permute-start.2 = (bf16[256,512]{1,0:T(8,128)(2,1)}, bf16[256,512]{1,0:T(8,128)(2,1)S(1)}, u32[]{:S(2)}, u32[]{:S(2)}) collective-permute-start(bf16[256,512]{1,0:T(8,128)(2,1)} %get-tuple-element.130), channel_id=1, source_target_pairs={{1,0},{0,1},{3,2},{2,3},{5,4},{4,5},{7,6},{6,7},{9,8},{8,9},{11,10... | collective-permute-start | bytes 786440 | tf_op jit(solution)/shard_map/ppermute | solution.py:293
  43.9 6.5 %copy-start.28 = (bf16[512,772]{0,1:T(8,128)(2,1)}, bf16[512,772]{0,1:T(8,128)(2,1)S(1)}, u32[]{:S(2)}) copy-start(bf16[512,772]{0,1:T(8,128)(2,1)S(1)} %collective-permute-done) | copy-start | bytes 2371588
  54.3 6.9 %copy-start = (f32[1024,896]{1,0:T(8,128)}, f32[1024,896]{1,0:T(8,128)S(1)}, u32[]{:S(2)}) copy-start(f32[1024,896]{1,0:T(8,128)S(1)} %fusion.48.proj_ref.prior_ref) | copy-start | bytes 11010052
  54.3 9.3 %copy-start.39 = (f32[256]{0:T(256)S(1)}, f32[256]{0:T(256)}, u32[]{:S(2)}) copy-start(f32[256]{0:T(256)} %param.32) | copy-start | bytes 3076
  80.4 2.4 copy-start.1
  80.4 2.6 copy-start.3
  80.4 2.8 copy-start.5
  82.5 18.5 %copy-start.30 = (bf16[1024,256]{1,0:T(8,128)(2,1)}, bf16[1024,256]{1,0:T(8,128)(2,1)S(1)}, u32[]{:S(2)}) copy-start(bf16[1024,256]{1,0:T(8,128)(2,1)S(1)} %get-tuple-element.108) | copy-start | bytes 1572868
  83.2 14.6 %copy-start.9 = (f32[1024,896]{0,1:T(8,128)S(1)}, f32[1024,896]{0,1:T(8,128)}, u32[]{:S(2)}) copy-start(f32[1024,896]{0,1:T(8,128)} %fusion.50) | copy-start | bytes 11010052
  83.2 14.6 %copy-start.49 = (bf16[1024,1024]{1,0:T(8,128)(2,1)S(1)}, bf16[1024,1024]{1,0:T(8,128)(2,1)}, u32[]{:S(2)}) copy-start(bf16[1024,1024]{1,0:T(8,128)(2,1)} %all-gather.3.cloned.1.call-done) | copy-start | bytes 6291460
  99.4 3.5 %copy-start.27 = (bf16[1024,640]{0,1:T(8,128)(2,1)}, bf16[1024,640]{0,1:T(8,128)(2,1)S(1)}, u32[]{:S(2)}) copy-start(bf16[1024,640]{0,1:T(8,128)(2,1)S(1)} %get-tuple-element.110) | copy-start | bytes 3932164
  104.5 3.7 %copy-start.13 = (bf16[512,256]{0,1:T(8,128)(2,1)S(1)}, bf16[512,256]{0,1:T(8,128)(2,1)}, u32[]{:S(2)}) copy-start(bf16[512,256]{0,1:T(8,128)(2,1)} %copy-done.12) | copy-start | bytes 786436
  104.5 3.7 %copy-start.24 = (bf16[512,256]{0,1:T(8,128)(2,1)S(1)}, bf16[512,256]{0,1:T(8,128)(2,1)}, u32[]{:S(2)}) copy-start(bf16[512,256]{0,1:T(8,128)(2,1)} %copy-done.23) | copy-start | bytes 786436
  104.5 3.7 %copy-start.26 = (bf16[512,256]{0,1:T(8,128)(2,1)S(1)}, bf16[512,256]{0,1:T(8,128)(2,1)}, u32[]{:S(2)}) copy-start(bf16[512,256]{0,1:T(8,128)(2,1)} %copy-done.25) | copy-start | bytes 786436
  104.5 3.7 %copy-start.29 = (bf16[512,772]{0,1:T(8,128)(2,1)S(1)}, bf16[512,772]{0,1:T(8,128)(2,1)}, u32[]{:S(2)}) copy-start(bf16[512,772]{0,1:T(8,128)(2,1)} %copy-done.28) | copy-start | bytes 2371588
  104.5 3.7 %copy-start.31 = (bf16[1024,256]{1,0:T(8,128)(2,1)S(1)}, bf16[1024,256]{1,0:T(8,128)(2,1)}, u32[]{:S(2)}) copy-start(bf16[1024,256]{1,0:T(8,128)(2,1)} %copy-done.30) | copy-start | bytes 1572868
  106.1 12.8 %collective-permute-start.13 = (f32[6,512]{1,0:T(8,128)S(1)}, f32[6,512]{1,0:T(8,128)S(1)}, u32[]{:S(2)}, u32[]{:S(2)}) collective-permute-start(f32[6,512]{1,0:T(8,128)S(1)} %fusion.35), channel_id=1, source_target_pairs={{1,0},{0,1},{3,2},{2,3},{5,4},{4,5},{7,6},{6,7},{9,8},{8,9},{11,10... | collective-permute-start | bytes 36872 | tf_op jit(solution)/shard_map/ppermute | solution.py:293
  106.5 25.4 %collective-permute-start.12 = (bf16[512,516]{0,1:T(8,128)(2,1)}, bf16[512,516]{0,1:T(8,128)(2,1)}, u32[]{:S(2)}, u32[]{:S(2)}) collective-permute-start(bf16[512,516]{0,1:T(8,128)(2,1)} %slice.234), channel_id=1, source_target_pairs={{1,0},{0,1},{3,2},{2,3},{5,4},{4,5},{7,6},{6,7},{9,8},{8,9},{11,10... | collective-permute-start | bytes 1585160 | tf_op jit(solution)/shard_map/ppermute | solution.py:293
  110.5 2.2 copy-start.11
  110.5 1.4 copy-start.37
  110.7 116.7 %collective-permute-start.7 = (bf16[2,256,1024]{2,1,0:T(8,128)(2,1)S(1)}, bf16[2,256,1024]{2,1,0:T(8,128)(2,1)}, u32[]{:S(2)}, u32[]{:S(2)}) collective-permute-start(bf16[2,256,1024]{2,1,0:T(8,128)(2,1)S(1)} %fusion.15), channel_id=1, source_target_pairs={{0,2},{2,0},{4,6},{6,4},{1,3},{3,1},{5,7},{7,5},{8,10},{10,8},{12,... | collective-permute-start | bytes 3145736 | tf_op jit(solution)/shard_map/ppermute | solution.py:309
  112.7 4.1 %copy-start.6 = (f32[1024,1024]{1,0:T(8,128)}, f32[1024,1024]{1,0:T(8,128)S(1)}, u32[]{:S(2)}) copy-start(f32[1024,1024]{1,0:T(8,128)S(1)} %fusion.32) | copy-start | bytes 12582916
  112.7 3.2 copy-start.14
  112.9 120.6 %collective-permute-start.3 = (bf16[2,256,1024]{2,1,0:T(8,128)(2,1)S(1)}, bf16[2,256,1024]{2,1,0:T(8,128)(2,1)}, u32[]{:S(2)}, u32[]{:S(2)}) collective-permute-start(bf16[2,256,1024]{2,1,0:T(8,128)(2,1)S(1)} %fusion.14), channel_id=1, source_target_pairs={{0,2},{2,0},{4,6},{6,4},{1,3},{3,1},{5,7},{7,5},{8,10},{10,8},{12,... | collective-permute-start | bytes 3145736 | tf_op jit(solution)/shard_map/ppermute | solution.py:309
  113.9 20.3 %collective-permute-start.15 = (bf16[512,256]{1,0:T(8,128)(2,1)}, bf16[512,256]{1,0:T(8,128)(2,1)}, u32[]{:S(2)}, u32[]{:S(2)}) collective-permute-start(bf16[512,256]{1,0:T(8,128)(2,1)} %get-tuple-element.120), channel_id=1, source_target_pairs={{1,0},{0,1},{3,2},{2,3},{5,4},{4,5},{7,6},{6,7},{9,8},{8,9},{11,10... | collective-permute-start | bytes 786440 | tf_op jit(solution)/shard_map/ppermute | solution.py:293
  118.8 13.0 %collective-permute-start.14 = (bf16[256,512]{1,0:T(8,128)(2,1)S(1)}, bf16[256,512]{1,0:T(8,128)(2,1)S(1)}, u32[]{:S(2)}, u32[]{:S(2)}) collective-permute-start(bf16[256,512]{1,0:T(8,128)(2,1)S(1)} %get-tuple-element.118), channel_id=1, source_target_pairs={{1,0},{0,1},{3,2},{2,3},{5,4},{4,5},{7,6},{6,7},{9,8},{8,9},{11,10... | collective-permute-start | bytes 786440 | tf_op jit(solution)/shard_map/ppermute | solution.py:293
  133.1 5.3 %copy-start.22 = (bf16[512,256]{0,1:T(8,128)(2,1)S(1)}, bf16[512,256]{0,1:T(8,128)(2,1)}, u32[]{:S(2)}) copy-start(bf16[512,256]{0,1:T(8,128)(2,1)} %slice.246) | copy-start | bytes 786436
  133.9 166.4 %all-reduce.11.cloned.1.call-start = ((), (), s32[]{:S(2)}) async-start(), calls=%async_computation.3 | async-start | bytes 3276800 | tf_op jit(solution)/shard_map/psum | solution.py:434
  138.4 88.3 %copy-start.40 = (f32[1024]{0:T(1024)S(1)}, f32[1024]{0:T(1024)}, u32[]{:S(2)}) copy-start(f32[1024]{0:T(1024)} %param.20) | copy-start | bytes 12292
  229.6 3.9 %copy-start.7 = (f32[1024,1024]{1,0:T(8,128)S(1)}, f32[1024,1024]{1,0:T(8,128)}, u32[]{:S(2)}) copy-start(f32[1024,1024]{1,0:T(8,128)} %copy-done.6) | copy-start | bytes 12582916
  229.8 10.2 %collective-permute-start.10 = (bf16[256,512]{1,0:T(8,128)(2,1)S(1)}, bf16[256,512]{1,0:T(8,128)(2,1)S(1)}, u32[]{:S(2)}, u32[]{:S(2)}) collective-permute-start(bf16[256,512]{1,0:T(8,128)(2,1)S(1)} %get-tuple-element.122), channel_id=1, source_target_pairs={{0,5},{1,4},{2,7},{3,6},{4,1},{5,0},{6,3},{7,2},{8,13},{9,12},{10,... | collective-permute-start | bytes 786440 | tf_op jit(solution)/shard_map/ppermute | solution.py:321
  231.6 13.9 %collective-permute-start.9 = (bf16[256,512]{1,0:T(8,128)(2,1)S(1)}, bf16[256,512]{1,0:T(8,128)(2,1)S(1)}, u32[]{:S(2)}, u32[]{:S(2)}) collective-permute-start(bf16[256,512]{1,0:T(8,128)(2,1)S(1)} %get-tuple-element.121), channel_id=1, source_target_pairs={{0,4},{1,5},{2,6},{3,7},{4,0},{5,1},{6,2},{7,3},{8,12},{9,13},{10,... | collective-permute-start | bytes 786440 | tf_op jit(solution)/shard_map/ppermute | solution.py:321
  232.9 12.7 %collective-permute-start.8 = (bf16[256,512]{1,0:T(8,128)(2,1)S(1)}, bf16[256,512]{1,0:T(8,128)(2,1)S(1)}, u32[]{:S(2)}, u32[]{:S(2)}) collective-permute-start(bf16[256,512]{1,0:T(8,128)(2,1)S(1)} %slice.311), channel_id=1, source_target_pairs={{0,1},{1,0},{2,3},{3,2},{4,5},{5,4},{6,7},{7,6},{8,9},{9,8},{10,11... | collective-permute-start | bytes 786440 | tf_op jit(solution)/shard_map/ppermute | solution.py:321
  235.4 10.2 %copy-start.8 = (f32[256,1024]{1,0:T(8,128)S(1)}, f32[256,1024]{1,0:T(8,128)}, u32[]{:S(2)}) copy-start(f32[256,1024]{1,0:T(8,128)} %param.18) | copy-start | bytes 3145732
  236.2 19.9 %collective-permute-start.6 = (bf16[256,512]{1,0:T(8,128)(2,1)}, bf16[256,512]{1,0:T(8,128)(2,1)}, u32[]{:S(2)}, u32[]{:S(2)}) collective-permute-start(bf16[256,512]{1,0:T(8,128)(2,1)} %get-tuple-element.124), channel_id=1, source_target_pairs={{0,5},{1,4},{2,7},{3,6},{4,1},{5,0},{6,3},{7,2},{8,13},{9,12},{10,... | collective-permute-start | bytes 786440 | tf_op jit(solution)/shard_map/ppermute | solution.py:321
  237.9 10.3 %copy-start.10 = (bf16[519,256]{0,1:T(8,128)(2,1)S(1)}, bf16[519,256]{0,1:T(8,128)(2,1)}, u32[]{:S(2)}) copy-start(bf16[519,256]{0,1:T(8,128)(2,1)} %all-reduce.9.cloned.1.call-done) | copy-start | bytes 797188
  237.9 18.3 %collective-permute-start.5 = (bf16[256,512]{1,0:T(8,128)(2,1)}, bf16[256,512]{1,0:T(8,128)(2,1)}, u32[]{:S(2)}, u32[]{:S(2)}) collective-permute-start(bf16[256,512]{1,0:T(8,128)(2,1)} %get-tuple-element.123), channel_id=1, source_target_pairs={{0,4},{1,5},{2,6},{3,7},{4,0},{5,1},{6,2},{7,3},{8,12},{9,13},{10,... | collective-permute-start | bytes 786440 | tf_op jit(solution)/shard_map/ppermute | solution.py:321
  239.9 5.7 %copy-start.19 = (bf16[256,512]{1,0:T(8,128)(2,1)}, bf16[256,512]{1,0:T(8,128)(2,1)S(1)}, u32[]{:S(2)}) copy-start(bf16[256,512]{1,0:T(8,128)(2,1)S(1)} %collective-permute-done.10) | copy-start | bytes 786436
  239.9 16.3 %collective-permute-start.4 = (bf16[256,512]{1,0:T(8,128)(2,1)}, bf16[256,512]{1,0:T(8,128)(2,1)}, u32[]{:S(2)}, u32[]{:S(2)}) collective-permute-start(bf16[256,512]{1,0:T(8,128)(2,1)} %slice.312), channel_id=1, source_target_pairs={{0,1},{1,0},{2,3},{3,2},{4,5},{5,4},{6,7},{7,6},{8,9},{9,8},{10,11... | collective-permute-start | bytes 786440 | tf_op jit(solution)/shard_map/ppermute | solution.py:321
  245.6 1.8 copy-start.21
  246.3 9.9 %collective-permute-start.11 = (f32[256]{0:T(256)S(1)}, f32[256]{0:T(256)S(1)}, u32[]{:S(2)}, u32[]{:S(2)}) collective-permute-start(f32[256]{0:T(256)S(1)} %multiply_reduce_fusion.4), channel_id=1, source_target_pairs={{1,0},{0,1},{3,2},{2,3},{5,4},{4,5},{7,6},{6,7},{9,8},{8,9},{11,10... | collective-permute-start | bytes 3080 | tf_op jit(solution)/shard_map/ppermute | solution.py:293
  300.3 4.5 %copy-start.18 = (bf16[2048,256]{1,0:T(8,128)(2,1)S(1)}, bf16[2048,256]{1,0:T(8,128)(2,1)}, u32[]{:S(2)}) copy-start(bf16[2048,256]{1,0:T(8,128)(2,1)} %get-tuple-element.104) | copy-start | bytes 3145732
  (6 other events, 5.5 us)
Sparse Core Ops, SparseCore 0:
  11.9 25.3 all-gather.2
  39.4 22.5 all-gather.4
  134.0 90.5 all-reduce.8
  228.1 72.1 all-reduce.10

commit v2 on v1

--- a/solution.py
+++ b/solution.py
@@ -323,6 +323,89 @@
     return total
 
 
+def sum_kernel(rows, cols, own_ref, out_ref, got, send_sem, recv_sem):
+    dp, row, col = lax.axis_index("dp"), lax.axis_index("row"), lax.axis_index("col")
+    peers = [
+        (dp, lax.rem(row + k // cols, rows), lax.rem(col + k % cols, cols)) for k in range(1, rows * cols)
+    ]
+    barrier = pltpu.get_barrier_semaphore()
+    for peer in peers:
+        pl.semaphore_signal(barrier, inc=1, device_id=peer, device_id_type=pl.DeviceIdType.MESH)
+    pl.semaphore_wait(barrier, len(peers))
+    copies = []
+    for k, peer in enumerate(peers):
+        copy = pltpu.make_async_remote_copy(
+            src_ref=own_ref,
+            dst_ref=got.at[k],
+            send_sem=send_sem.at[k],
+            recv_sem=recv_sem.at[k],
+            device_id=peer,
+            device_id_type=pl.DeviceIdType.MESH,
+        )
+        copy.start()
+        copies.append(copy)
+    for copy in copies:
+        copy.wait()
+    total = own_ref[...]
+    for k in range(len(peers)):
+        total = total + got[k]
+    out_ref[...] = total
+
+
+def sum_over_group(values):
+    rows, cols = lax.axis_size("row"), lax.axis_size("col")
+    others = rows * cols - 1
+    return pl.pallas_call(
+        functools.partial(sum_kernel, rows, cols),
+        out_shape=jax.ShapeDtypeStruct(values.shape, values.dtype),
+        in_specs=[pl.BlockSpec(memory_space=pltpu.VMEM)],
+        out_specs=pl.BlockSpec(memory_space=pltpu.VMEM),
+        scratch_shapes=[
+            pltpu.VMEM((others, *values.shape), values.dtype),
+            pltpu.SemaphoreType.DMA((others,)),
+            pltpu.SemaphoreType.DMA((others,)),
+        ],
+        compiler_params=pltpu.CompilerParams(collective_id=0, has_side_effects=True),
+        name="sum_over_group",
+    )(values)
+
+
+def dp_scatter(matrix):
+    count = lax.axis_size("dp")
+    index = lax.axis_index("dp")
+    unit = count * 16
+    rows = -(-matrix.shape[0] // unit) * unit
+    blocks = pad_to(matrix, rows, matrix.shape[1]).reshape(count, rows // count, matrix.shape[1])
+    total = lax.dynamic_index_in_dim(blocks, index, 0, keepdims=False).astype(F32)
+    for k in range(1, count):
+        send = lax.dynamic_index_in_dim(blocks, (index + k) % count, 0, keepdims=False)
+        pairs = [(i, (i + k) % count) for i in range(count)]
+        total = total + lax.ppermute(send, "dp", pairs).astype(F32)
+    return total.astype(BF16)
+
+
+def dp_gather(pieces):
+    every = lax.all_gather(jnp.concatenate(pieces, axis=0), "dp", axis=0, tiled=False)
+    got, at = [], 0
+    for piece in pieces:
+        part = every[:, at : at + piece.shape[0]]
+        got.append(part.reshape(-1, piece.shape[1]))
+        at += piece.shape[0]
+    return got
+
+
+def row_sum(matrix):
+    count = lax.axis_size("row")
+    if count & (count - 1):
+        return lax.psum(matrix.astype(F32), "row").astype(BF16)
+    bit = 1
+    while bit < count:
+        other = lax.ppermute(matrix, "row", [(i, i ^ bit) for i in range(count)])
+        matrix = (matrix.astype(F32) + other.astype(F32)).astype(BF16)
+        bit *= 2
+    return matrix
+
+
 def pad_to(matrix, rows, columns):
     return jnp.pad(matrix, ((0, rows - matrix.shape[0]), (0, columns - matrix.shape[1])))
 
@@ -371,13 +454,14 @@
 
     weights = jnp.concatenate(from_columns(weights_for), axis=0)
     weights = jnp.pad(weights, ((0, 0), (0, LANES - heads)))
+    weights, cot_later, out_weight = lax.optimization_barrier((weights, cotangent, out_weight))
 
     def out_rows_for(k):
         split = out_weight.reshape(col_count, chan, out_weight.shape[1])
         return lax.dynamic_index_in_dim(split, (col_index + k) % col_count, 0, keepdims=False)
 
     out_own = jnp.concatenate(from_columns(out_rows_for), axis=1)
-    cot_half = cotangent.astype(BF16)
+    cot_half = cot_later.astype(BF16)
     cot_wide = jnp.concatenate(from_columns(lambda k: cot_half), axis=1)
 
     inv_rms = lax.rsqrt(jnp.mean(hidden * hidden, axis=1, keepdims=True) + EPSILON)
@@ -402,8 +486,8 @@
 
     grad_gate_out = dot_nt(cot_rows, out_own)
     grad_hat = grad_gate_out * gate_gain[None, :]
-    sums = lax.psum(
-        jnp.stack([jnp.sum(gated * gated, axis=1), jnp.sum(grad_hat * gated, axis=1)]), ("row", "col")
+    sums = sum_over_group(
+        jnp.stack([jnp.sum(gated * gated, axis=1), jnp.sum(grad_hat * gated, axis=1)])
     )
     inv_gate = lax.rsqrt(sums[0] / inner + EPSILON)[:, None]
     gate_dot = sums[1][:, None] * inv_gate
@@ -416,6 +500,9 @@
     gate_out = (gate_hat * gate_gain[None, :]).astype(BF16)
     grad_gate_gain = jnp.sum(grad_gate_out * gate_hat, axis=0)
 
+    out_part = dot_tn(gate_out, cot_rows)
+    z_part = dot_tn(gathered, grad_z)
+    grad_mixed, out_part, z_part = lax.optimization_barrier((grad_mixed, out_part, z_part))
     slots, conv_grads, head_grads, skip_grads = mixer_backward(
         proj, conv_pack, head_pack, mixed, inside, states, grad_mixed, heads, head_width, wide
     )
@@ -426,12 +513,12 @@
     def in_col_order(relative, axis):
         return jnp.roll(relative, col_index, axis)
 
-    out_part = dot_tn(gate_out, cot_rows)
     out_rel = from_columns(lambda k: out_part[:, k * width : (k + 1) * width].astype(BF16))
-    z_part = dot_tn(gathered, grad_z)
     z_blocks = to_col_blocks(z_part)
     z_rel = from_columns(lambda k: z_blocks[k].astype(BF16))
-    early = lax.psum(jnp.concatenate([piece.reshape(-1, chan) for piece in out_rel + z_rel], axis=0), "dp")
+    (early,) = dp_gather(
+        [dp_scatter(jnp.concatenate([piece.reshape(-1, chan) for piece in out_rel + z_rel], axis=0))]
+    )
     out_size = chan * width // chan
     out_sum = early[: out_size * col_count].reshape(col_count, chan, width)
     z_sum = early[out_size * col_count :].reshape(col_count, width, chan)
@@ -448,9 +535,8 @@
     grad_scaled = scatter_sum(dot_nt(grad_slots, weights))
 
     late_part = dot_tn(gathered, slots)
-    weights_f32 = weights.astype(F32)
-    gain_part = jnp.sum(z_part * weights_f32[:, :chan], axis=1) + jnp.sum(
-        late_part * weights_f32[:, chan:], axis=1
+    gain_part = jnp.sum(z_part * weights[:, :chan].astype(F32), axis=1) + jnp.sum(
+        late_part * weights[:, chan:].astype(F32), axis=1
     )
     late_blocks = to_col_blocks(late_part[:, : wide + heads])
     gain_blocks = gain_part.reshape(col_count, 1, width)
@@ -473,16 +559,15 @@
         grad_gate_gain[None, :].astype(BF16),
         pad_to(head_row, 1, chan).astype(BF16),
     ]
-    late = lax.psum(jnp.concatenate(dp_rows, axis=0), "dp")
+    x_piece = dp_scatter(jnp.concatenate(dp_rows, axis=0))
     bc_mine = sum(piece[:, chan:wide].astype(F32) for piece in late_rel).astype(BF16)
-    small_mine = sum(small_rel)
-    shared = lax.psum(
-        jnp.concatenate(
-            [bc_mine, small_mine[:5, :bc_width].astype(BF16), small_mine[5].reshape(-1, bc_width).astype(BF16)],
-            axis=0,
-        ),
-        ("dp", "row"),
-    ).astype(F32)
+    small_mine = sum(small_rel).astype(BF16)
+    shared_rows = jnp.concatenate(
+        [bc_mine, small_mine[:5, :bc_width], small_mine[5].reshape(-1, bc_width)], axis=0
+    )
+    bc_piece = dp_scatter(row_sum(shared_rows))
+    late, shared = dp_gather([x_piece, bc_piece])
+    shared = shared.astype(F32)
 
     dt_count = width * heads // chan
     x_sum = late[: width * col_count].reshape(col_count, width, chan)
@@ -497,7 +582,7 @@
     rest = late[at + dt_count * col_count :].astype(F32)
     grad_weight_bc = shared[:width]
     gain_col = lax.dynamic_slice_in_dim(norm_gain, col_index * width, width, 0)
-    grad_norm_gain = shared[width + 5 :].reshape(-1) / gain_col
+    grad_norm_gain = shared[width + 5 : width + 5 + width // bc_width].reshape(-1) / gain_col
 
     normed_col = hidden_col * inv_rms
     grad_in = grad_scaled * gain_col[None, :]

time: 322 us -> 259 us (0.80)
  waiting for transfers between devices: 170 us -> 58 us
  starting transfers between devices: 18.2 us -> 36.6 us
  local copies, waits for them, and re-layouts: 35.9 us -> 49.2 us
  Pallas kernels: 21.4 us -> 28 us
  matrix products: 13.8 us -> 19.8 us
  blocking collectives: 14.3 us -> 18.4 us
    psum x2 -> x0, waiting for transfers between devices: 126 us -> none  [the longest x1 85.2 us: body(): lax.psum(jnp.concatenate([bc_mine, small_mine[:5, :bc_width].astype(BF16)...]
    ppermute x0 -> x11, waiting for transfers between devices: none -> 25 us  [the longest x9 23.2 us: dp_scatter(): total = total + lax.ppermute(send, 'dp', pairs).astype(F32)]
    all_gather x0 -> x1, blocking collectives: none -> 18.4 us  [dp_gather(): lax.all_gather(jnp.concatenate(pieces, axis=0), 'dp', axis=0, tiled=False)]
    ppermute x0 -> x11, starting transfers between devices: none -> 17.5 us  [the longest x9 16.8 us: dp_scatter(): total = total + lax.ppermute(send, 'dp', pairs).astype(F32)]
    ppermute x8, waiting for transfers between devices: 38.7 us -> 23.3 us  [from_columns(): got.append(lax.ppermute(block_for((count - j) % count), 'col', pairs))]
    psum x1 -> x0, blocking collectives: 14.3 us -> none  [body(): lax.psum(jnp.stack([jnp.sum(gated * gated, axis=1), jnp.sum(grad_hat * ga...]
    all_gather x1, waiting for transfers between devices: 0.01 us -> 9.59 us  [body(): cot_rows = lax.all_gather(cot_wide, 'row', axis=0, tiled=True)]
    pallas_call x0 -> x1, Pallas kernels: none -> 6.09 us  [sum_over_group(): pl.pallas_call(functools.partial(sum_kernel, rows, cols), out_shape=jax.S...]
  transfers between devices with their start and end apart: 20 -> 30, of which waited for: 9 -> 8; matrix products, arithmetic and copies ran while one was open for 14% -> 26% of each run, Pallas kernels for 2% -> 3%
where the time goes in v2:
time: 259 us; the launch traced here: 258 us
  waiting for transfers between devices  58 us (22%)
  local copies, waits for them, and re-layouts  49.2 us (19%)
  starting transfers between devices  36.6 us (14%)
  other arithmetic  33 us (13%)
  Pallas kernels  28 us (11%)
  matrix products  19.8 us (8%)
  blocking collectives  18.4 us (7%)
  between operations  14.9 us (6%)
    ppermute x8, waiting for transfers between devices, from_columns(): got.append(lax.ppermute(block_for((count - j) % count), 'col', pairs))  23.3 us
    ppermute x9, waiting for transfers between devices, dp_scatter(): total = total + lax.ppermute(send, 'dp', pairs).astype(F32)  23.2 us
    all_gather x1, blocking collectives, dp_gather(): lax.all_gather(jnp.concatenate(pieces, axis=0), 'dp', axis=0, tiled=False)  18.4 us
    ppermute x9, starting transfers between devices, dp_scatter(): total = total + lax.ppermute(send, 'dp', pairs).astype(F32)  16.8 us
    pallas_call x1, Pallas kernels, mixer_backward(): pl.pallas_call(functools.partial(backward_kernel, heads, head_width), gri...  15.1 us
    ppermute x8, starting transfers between devices, from_columns(): got.append(lax.ppermute(block_for((count - j) % count), 'col', pairs))  11 us
    all_gather x1, waiting for transfers between devices, body(): cot_rows = lax.all_gather(cot_wide, 'row', axis=0, tiled=True)  9.59 us
    unnamed x91, local copies, waits for them, and re-layouts  8.2 us
  transfers between devices with their start and end apart: 30, of which 8 were waited for; matrix products, arithmetic and copies ran while one was open for 26% of the time, Pallas kernels for 3%

profile of v2, /device:TPU:0, one launch (start us, length us, event | category | flops | bytes accessed | tf_op | source)
XLA Modules:
  0.0 257.9 jit_solution(725846296932761629)
XLA Ops:
  7.3 1.4 multiply_reduce_fusion.5
  9.6 2.2 fusion.18
  12.4 2.2 constant_dynamic-slice_fusion.4
  16.0 3.1 %collective-permute-start = (bf16[512,772]{0,1:T(8,128)(2,1)S(1)}, bf16[512,772]{0,1:T(8,128)(2,1)}, u32[]{:S(2)}, u32[]{:S(2)}) collective-permute-start(bf16[512,772]{0,1:T(8,128)(2,1)S(1)} %pad_maximum_fusion.1), channel_id=1, source_target_pairs={{1,0},{0,1},{3,2},{2,3},{5,4},{4,5},{7,6},{6,7},{9,8},{8,9},{11,10... | collective-permute-start | bytes 2371592 | tf_op jit(solution)/shard_map/ppermute | solution.py:293
  19.3 17.5 %collective-permute-done = bf16[512,772]{0,1:T(8,128)(2,1)} collective-permute-done((bf16[512,772]{0,1:T(8,128)(2,1)S(1)}, bf16[512,772]{0,1:T(8,128)(2,1)}, u32[]{:S(2)}, u32[]{:S(2)}) %collective-permute-start) | collective-permute-done | bytes 790560 | tf_op jit(solution)/shard_map/ppermute | solution.py:293
  36.9 1.5 copy.122
  38.4 1.2 fusion.8
  39.7 1.8 collective-permute-start.1
  41.5 5.7 %collective-permute-done.1 = bf16[256,512]{1,0:T(8,128)(2,1)S(1)} collective-permute-done((bf16[256,512]{1,0:T(8,128)(2,1)S(1)}, bf16[256,512]{1,0:T(8,128)(2,1)S(1)}, u32[]{:S(2)}, u32[]{:S(2)}) %collective-permute-start.1) | collective-permute-done | bytes 262176 | tf_op jit(solution)/shard_map/ppermute | solution.py:293
  49.4 1.5 collective-permute-start.2
  50.9 3.9 %fusion.64.proj_ref.prior_ref = f32[1024,896]{1,0:T(8,128)S(1)} fusion(bf16[1024,1024]{1,0:T(8,128)(2,1)} %all-gather.6.cloned.1.call-done, bf16[1024,896]{1,0:T(8,128)(2,1)S(1)} %fusion.8), kind=kOutput, calls=%fused_computation.163 | convolution fusion | flops 1879048192 | bytes 7602176 | tf_op jit(solution)/shard_map/dot_general | solution.py:471
  54.8 6.9 %mixer_forward.1 = (f32[1024,256]{1,0:T(8,128)S(1)}, f32[1024,256]{1,0:T(8,128)S(1)}, f32[1024,256]{1,0:T(8,128)S(1)}, f32[4,128,256]{2,1,0:T(8,128)S(1)}) custom-call(f32[1024,896]{1,0:T(8,128)S(1)} %fusion.64.proj_ref.prior_ref, f32[8,512]{1,0:T(8,128)S(1)} %select_maximum_fusion.conv_ref, f32[8,128]{1,0:T(8,128)S(1)} %select_maximum_fusion.2.head_ref), custom_call_target="tpu_custom_call" | custom-call | flops 4000000000 | bytes 7340032 | tf_op jit(solution)/shard_map/mixer_forward/pallas_call | solution.py:225
  62.5 9.6 %all-gather.8.cloned.1.call-done = bf16[1024,1024]{1,0:T(8,128)(2,1)} async-done(((bf16[256,1024]{1,0:T(8,128)(2,1)}), bf16[1024,1024]{1,0:T(8,128)(2,1)}) %all-gather.8.cloned.1.call-update) | async-done | bytes 2097168 | tf_op jit(solution)/shard_map/all_gather | solution.py:470
  72.1 3.3 %multiply_reduce_fusion.4 = (f32[1024]{0:T(1024)S(1)}, f32[1024]{0:T(1024)S(1)}, f32[1024,256]{1,0:T(8,128)}) fusion(f32[1024,256]{1,0:T(8,128)S(1)} %get-tuple-element.32, f32[256]{0:T(256)S(1)} %copy-done.29, bf16[1024,1024]{1,0:T(8,128)(2,1)} %all-gather.8.cloned.1.call-done, bf16[256,512]{1,0:T(8,128)(2,1)} %collective-permute-done.2, ...), kind=kOutput, calls=%fused_computation.47 | convolution fusion | flops 539228160 | bytes 4727808 | tf_op jit(solution)/shard_map/dot_general | solution.py:29
  76.0 6.1 %sum_over_group.1 = f32[2,1024]{1,0:T(2,128)} custom-call(f32[2,1024]{1,0:T(2,128)} %pad_maximum_fusion.8.own_ref), custom_call_target="tpu_custom_call" | custom-call | tf_op jit(solution)/shard_map/sum_over_group/pallas_call | solution.py:358
  82.9 2.4 multiply_convert_fusion
  85.4 1.7 fusion.52
  87.0 1.7 fusion.65
  89.6 15.1 %mixer_backward.1 = (bf16[1024,640]{1,0:T(8,128)(2,1)S(1)}, f32[8,512]{1,0:T(8,128)S(1)}, f32[8,128]{1,0:T(8,128)S(1)}, f32[8,256]{1,0:T(8,128)S(1)}) custom-call(f32[1024,896]{1,0:T(8,128)S(1)} %copy-done.1, f32[1024,896]{1,0:T(8,128)S(1)} %copy-done.1, f32[8,512]{1,0:T(8,128)S(1)} %select_maximum_fusion.conv_ref, ...), custom_call_target="tpu_custom_call" | custom-call | flops 12000000000 | bytes 9437184 | tf_op jit(solution)/shard_map/mixer_backward/pallas_call | solution.py:252
  104.7 3.1 %fusion.63 = (bf16[1024,640]{0,1:T(8,128)(2,1)S(1)}, f32[1024,640]{0,1:T(8,128)}) fusion(bf16[1024,1024]{1,0:T(8,128)(2,1)S(1)} %copy-done.39, bf16[1024,640]{1,0:T(8,128)(2,1)S(1)} %get-tuple-element.39), kind=kOutput, calls=%fused_computation.162 | convolution fusion | flops 1342832640 | bytes 7340032 | tf_op jit(solution)/shard_map/dot_general | solution.py:33
  108.5 4.4 %fusion.9 = f32[1024,1024]{1,0:T(8,128)} fusion(bf16[1024,896]{1,0:T(8,128)(2,1)S(1)} %copy-done.8, bf16[1024,640]{1,0:T(8,128)(2,1)S(1)} %get-tuple-element.39, bf16[1024,256]{1,0:T(8,128)(2,1)S(1)} %get-tuple-element.49), kind=kOutput, calls=%fused_computation.17 | convolution fusion | flops 1882718208 | bytes 7864320 | tf_op jit(solution)/shard_map/dot_general | solution.py:29
  114.7 1.5 collective-permute-start.22
  116.2 1.9 fusion.55
  119.4 3.3 %copy.139 = f32[1024,640]{1,0:T(8,128)} copy(f32[1024,640]{0,1:T(8,128)} %get-tuple-element.96) | data formatting | bytes 5242880 | tf_op jit(solution)/shard_map/dot_general | solution.py:33
  122.7 2.1 multiply_reduce_fusion
  124.8 1.5 collective-permute-start.16
  128.0 1.7 fusion.14
  129.9 1.7 fusion.34
  131.6 2.0 copy-done.4
  133.6 1.1 fusion.13
  138.2 1.0 reshape.192
  139.2 1.0 pad_maximum_fusion
  141.2 1.5 collective-permute-start.24
  142.7 2.3 collective-permute-start.26
  145.6 1.1 add_convert_fusion.2
  149.5 1.1 concatenate.80
  150.9 1.7 pad_maximum_fusion.6
  153.4 8.5 %collective-permute-start.13 = (bf16[272,256]{1,0:T(8,128)(2,1)}, bf16[272,256]{1,0:T(8,128)(2,1)}, u32[]{:S(2)}, u32[]{:S(2)}) collective-permute-start(bf16[272,256]{1,0:T(8,128)(2,1)} %get-tuple-element.61), channel_id=1, source_target_pairs={{0,8},{8,16},{16,24},{24,0},{1,9},{9,17},{17,25},{25,1},{2,10},{10... | collective-permute-start | bytes 417800 | tf_op jit(solution)/shard_map/ppermute | solution.py:383
  161.9 10.0 %collective-permute-done.25 = bf16[512,256]{1,0:T(8,128)(2,1)} collective-permute-done((bf16[512,256]{1,0:T(8,128)(2,1)}, bf16[512,256]{1,0:T(8,128)(2,1)}, u32[]{:S(2)}, u32[]{:S(2)}) %collective-permute-start.25) | collective-permute-done | bytes 262176 | tf_op jit(solution)/shard_map/ppermute | solution.py:383
  171.9 1.9 fusion.33
  174.0 6.8 %collective-permute-done.14 = bf16[272,256]{1,0:T(8,128)(2,1)} collective-permute-done((bf16[272,256]{1,0:T(8,128)(2,1)S(1)}, bf16[272,256]{1,0:T(8,128)(2,1)}, u32[]{:S(2)}, u32[]{:S(2)}) %collective-permute-start.14) | collective-permute-done | bytes 139296 | tf_op jit(solution)/shard_map/ppermute | solution.py:383
  180.8 1.8 fusion.38
  183.4 2.2 bitcast_add_fusion
  186.4 1.5 collective-permute-start.8
  188.8 1.5 collective-permute-start.9
  191.5 1.9 collective-permute-done.18
  195.4 3.8 %collective-permute-start.21 = (bf16[144,256]{1,0:T(8,128)(2,1)S(1)}, bf16[144,256]{1,0:T(8,128)(2,1)S(1)}, u32[]{:S(2)}, u32[]{:S(2)}) collective-permute-start(bf16[144,256]{1,0:T(8,128)(2,1)S(1)} %get-tuple-element.79), channel_id=1, source_target_pairs={{0,24},{8,0},{16,8},{24,16},{1,25},{9,1},{17,9},{25,17},{2,26},{10... | collective-permute-start | bytes 221192 | tf_op jit(solution)/shard_map/ppermute | solution.py:383
  200.1 3.8 %collective-permute-done.19 = bf16[144,256]{1,0:T(8,128)(2,1)S(1)} collective-permute-done((bf16[144,256]{1,0:T(8,128)(2,1)S(1)}, bf16[144,256]{1,0:T(8,128)(2,1)S(1)}, u32[]{:S(2)}, u32[]{:S(2)}) %collective-permute-start.19) | collective-permute-done | bytes 73760 | tf_op jit(solution)/shard_map/ppermute | solution.py:383
  203.9 1.5 collective-permute-start.10
  205.5 2.6 collective-permute-done.20
  208.1 1.5 collective-permute-start.5
  209.6 18.4 %all-gather = bf16[1664,256]{1,0:T(8,128)(2,1)S(1)} all-gather(bf16[416,256]{1,0:T(8,128)(2,1)S(1)} %pad_maximum_fusion.7), channel_id=2, replica_groups=mesh['dp'=4,'row'=4,'col'=2] {'dp'}, dimensions={0}, use_global_device_ids=true | all-gather | bytes 1064960 | tf_op jit(solution)/shard_map/all_gather | solution.py:388
  229.8 1.3 reshape.196
  231.0 1.1 copy.146
  232.7 1.6 collective-permute-start.6
  234.4 1.3 multiply_reduce_fusion.6
  236.9 1.3 slice.266
  238.1 1.3 slice.265
  240.9 1.1 copy.159
  242.6 2.6 %multiply_add_fusion = (f32[256,512]{1,0:T(8,128)}, f32[256,512]{1,0:T(8,128)}) fusion(f32[256,512]{1,0:T(8,128)S(1)} %copy-done.16, f32[256,1024]{1,0:T(8,128)S(1)} %copy-done.6, s32[]{:T(128)S(6)} %select_n.169, f32[256]{0:T(256)S(1)} %add_multiply_fusion, f32[256]{0:T(256)S(1)} %add_rsqrt_fusion.1, f32[512]{0:T(512)S(1)} %get-tuple-element.48, ...), kind=kLoop, calls=%fused_computation.76 | loop fusion | flops 2490368 | bytes 4722692 | tf_op jit(solution)/shard_map/add | solution.py:590
  245.2 1.3 fusion.54
  247.4 1.8 fusion.24
  249.2 1.0 copy.161
  250.2 1.1 bitcast_convert_fusion.2
  (217 shorter events, 35.8 us)
Async XLA Ops:
  7.2 4.7 %copy-start.31 = (bf16[512,8]{0,1:T(8,128)(2,1)S(1)}, bf16[512,8]{0,1:T(8,128)(2,1)}, u32[]{:S(2)}) copy-start(bf16[512,8]{0,1:T(8,128)(2,1)} %param.23) | copy-start | bytes 24580
  7.2 4.7 %copy-start.17 = (bf16[512,256]{1,0:T(8,128)(2,1)S(1)}, bf16[512,256]{1,0:T(8,128)(2,1)}, u32[]{:S(2)}) copy-start(bf16[512,256]{1,0:T(8,128)(2,1)} %param.24) | copy-start | bytes 786436
  7.2 4.9 %copy-start.27 = (bf16[512,512]{1,0:T(8,128)(2,1)S(1)}, bf16[512,512]{1,0:T(8,128)(2,1)}, u32[]{:S(2)}) copy-start(bf16[512,512]{1,0:T(8,128)(2,1)} %param.21) | copy-start | bytes 1572868
  7.2 43.6 %all-gather.6.cloned.1.call-start = ((), (), s32[]{:S(2)}) async-start(), calls=%async_computation | async-start | bytes 2621440 | tf_op jit(solution)/shard_map/all_gather | solution.py:469
  8.7 3.5 %copy-start.28 = (bf16[512,512]{1,0:T(8,128)(2,1)S(1)}, bf16[512,512]{1,0:T(8,128)(2,1)}, u32[]{:S(2)}) copy-start(bf16[512,512]{1,0:T(8,128)(2,1)} %param.22) | copy-start | bytes 1572868
  11.8 60.2 %all-gather.8.cloned.1.call-start = ((), (), s32[]{:S(2)}) async-start(), calls=%async_computation.1 | async-start | bytes 2621440 | tf_op jit(solution)/shard_map/all_gather | solution.py:470
  16.0 20.9 %collective-permute-start = (bf16[512,772]{0,1:T(8,128)(2,1)S(1)}, bf16[512,772]{0,1:T(8,128)(2,1)}, u32[]{:S(2)}, u32[]{:S(2)}) collective-permute-start(bf16[512,772]{0,1:T(8,128)(2,1)S(1)} %pad_maximum_fusion.1), channel_id=1, source_target_pairs={{1,0},{0,1},{3,2},{2,3},{5,4},{4,5},{7,6},{6,7},{9,8},{8,9},{11,10... | collective-permute-start | bytes 2371592 | tf_op jit(solution)/shard_map/ppermute | solution.py:293
  39.6 11.3 %copy-start.7 = (bf16[1024,896]{1,0:T(8,128)(2,1)}, bf16[1024,896]{1,0:T(8,128)(2,1)S(1)}, u32[]{:S(2)}) copy-start(bf16[1024,896]{1,0:T(8,128)(2,1)S(1)} %fusion.8) | copy-start | bytes 5505028
  39.6 8.9 %copy-start.34 = (f32[256]{0:T(256)S(1)}, f32[256]{0:T(256)}, u32[]{:S(2)}) copy-start(f32[256]{0:T(256)} %param.28) | copy-start | bytes 3076
  39.6 8.9 %copy-start.35 = (f32[256]{0:T(256)S(1)}, f32[256]{0:T(256)}, u32[]{:S(2)}) copy-start(f32[256]{0:T(256)} %param.26) | copy-start | bytes 3076
  39.6 8.9 %copy-start.36 = (f32[4]{0:T(128)S(1)}, f32[4]{0:T(128)}, u32[]{:S(2)}) copy-start(f32[4]{0:T(128)} %param.31) | copy-start | bytes 52
  39.6 8.9 %copy-start.37 = (f32[4]{0:T(128)S(1)}, f32[4]{0:T(128)}, u32[]{:S(2)}) copy-start(f32[4]{0:T(128)} %param.30) | copy-start | bytes 52
  39.6 8.9 %copy-start.38 = (f32[4]{0:T(128)S(1)}, f32[4]{0:T(128)}, u32[]{:S(2)}) copy-start(f32[4]{0:T(128)} %param.29) | copy-start | bytes 52
  39.7 8.9 %copy-start.32 = (f32[4,256]{1,0:T(4,128)S(1)}, f32[4,256]{1,0:T(4,128)}, u32[]{:S(2)}) copy-start(f32[4,256]{1,0:T(4,128)} %param.27) | copy-start | bytes 12292
  39.7 8.9 %copy-start.33 = (f32[4,256]{1,0:T(4,128)S(1)}, f32[4,256]{1,0:T(4,128)}, u32[]{:S(2)}) copy-start(f32[4,256]{1,0:T(4,128)} %param.25) | copy-start | bytes 12292
  39.7 9.0 %copy-start.26 = (bf16[512,512]{1,0:T(8,128)(2,1)S(1)}, bf16[512,512]{1,0:T(8,128)(2,1)}, u32[]{:S(2)}) copy-start(bf16[512,512]{1,0:T(8,128)(2,1)} %param.33) | copy-start | bytes 1572868
  39.7 7.5 %collective-permute-start.1 = (bf16[256,512]{1,0:T(8,128)(2,1)S(1)}, bf16[256,512]{1,0:T(8,128)(2,1)S(1)}, u32[]{:S(2)}, u32[]{:S(2)}) collective-permute-start(bf16[256,512]{1,0:T(8,128)(2,1)S(1)} %convert_element_type.224), channel_id=1, source_target_pairs={{1,0},{0,1},{3,2},{2,3},{5,4},{4,5},{7,6},{6,7},{9,8},{8,9},{11,10... | collective-permute-start | bytes 786440 | tf_op jit(solution)/shard_map/ppermute | solution.py:293
  48.2 197.1 %all-gather.10.cloned.1.call-start = ((), (), s32[]{:S(2)}) async-start(), calls=%async_computation.2 | async-start | bytes 1310720 | tf_op jit(solution)/shard_map/all_gather | solution.py:388
  49.4 22.7 %copy-start.18 = (bf16[256,512]{1,0:T(8,128)(2,1)}, bf16[256,512]{1,0:T(8,128)(2,1)S(1)}, u32[]{:S(2)}) copy-start(bf16[256,512]{1,0:T(8,128)(2,1)S(1)} %get-tuple-element.72) | copy-start | bytes 786436
  49.4 13.1 %collective-permute-start.2 = (bf16[256,512]{1,0:T(8,128)(2,1)}, bf16[256,512]{1,0:T(8,128)(2,1)}, u32[]{:S(2)}, u32[]{:S(2)}) collective-permute-start(bf16[256,512]{1,0:T(8,128)(2,1)} %get-tuple-element.73), channel_id=1, source_target_pairs={{1,0},{0,1},{3,2},{2,3},{5,4},{4,5},{7,6},{6,7},{9,8},{8,9},{11,10... | collective-permute-start | bytes 786440 | tf_op jit(solution)/shard_map/ppermute | solution.py:293
  54.8 6.9 %copy-start = (f32[1024,896]{1,0:T(8,128)}, f32[1024,896]{1,0:T(8,128)S(1)}, u32[]{:S(2)}) copy-start(f32[1024,896]{1,0:T(8,128)S(1)} %fusion.64.proj_ref.prior_ref) | copy-start | bytes 11010052
  54.8 17.3 %copy-start.29 = (f32[256]{0:T(256)S(1)}, f32[256]{0:T(256)}, u32[]{:S(2)}) copy-start(f32[256]{0:T(256)} %param.32) | copy-start | bytes 3076
  82.9 2.5 copy-start.14
  87.0 2.4 copy-start.1
  87.0 2.5 copy-start.3
  104.7 3.9 %copy-start.8 = (bf16[1024,896]{1,0:T(8,128)(2,1)S(1)}, bf16[1024,896]{1,0:T(8,128)(2,1)}, u32[]{:S(2)}) copy-start(bf16[1024,896]{1,0:T(8,128)(2,1)} %copy-done.7) | copy-start | bytes 5505028
  107.8 5.1 %copy-start.23 = (bf16[1024,640]{0,1:T(8,128)(2,1)}, bf16[1024,640]{0,1:T(8,128)(2,1)S(1)}, u32[]{:S(2)}) copy-start(bf16[1024,640]{0,1:T(8,128)(2,1)S(1)} %get-tuple-element.95) | copy-start | bytes 3932164
  108.5 5.3 %copy-start.13 = (bf16[256,1024]{1,0:T(8,128)(2,1)S(1)}, bf16[256,1024]{1,0:T(8,128)(2,1)}, u32[]{:S(2)}) copy-start(bf16[256,1024]{1,0:T(8,128)(2,1)} %fusion.52) | copy-start | bytes 1572868
  114.7 23.5 %collective-permute-start.22 = (bf16[256,512]{1,0:T(8,128)(2,1)}, bf16[256,512]{1,0:T(8,128)(2,1)}, u32[]{:S(2)}, u32[]{:S(2)}) collective-permute-start(bf16[256,512]{1,0:T(8,128)(2,1)} %get-tuple-element.65), channel_id=1, source_target_pairs={{1,0},{0,1},{3,2},{2,3},{5,4},{4,5},{7,6},{6,7},{9,8},{8,9},{11,10... | collective-permute-start | bytes 786440 | tf_op jit(solution)/shard_map/ppermute | solution.py:293
  118.9 20.3 %collective-permute-start.23 = (bf16[512,256]{1,0:T(8,128)(2,1)}, bf16[512,256]{1,0:T(8,128)(2,1)}, u32[]{:S(2)}, u32[]{:S(2)}) collective-permute-start(bf16[512,256]{1,0:T(8,128)(2,1)} %get-tuple-element.67), channel_id=1, source_target_pairs={{1,0},{0,1},{3,2},{2,3},{5,4},{4,5},{7,6},{6,7},{9,8},{8,9},{11,10... | collective-permute-start | bytes 786440 | tf_op jit(solution)/shard_map/ppermute | solution.py:293
  124.8 5.1 %copy-start.19 = (bf16[256,512]{1,0:T(8,128)(2,1)S(1)}, bf16[256,512]{1,0:T(8,128)(2,1)}, u32[]{:S(2)}) copy-start(bf16[256,512]{1,0:T(8,128)(2,1)} %copy-done.18) | copy-start | bytes 786436
  124.8 12.4 %collective-permute-start.16 = (f32[6,512]{1,0:T(8,128)S(1)}, f32[6,512]{1,0:T(8,128)S(1)}, u32[]{:S(2)}, u32[]{:S(2)}) collective-permute-start(f32[6,512]{1,0:T(8,128)S(1)} %fusion.43), channel_id=1, source_target_pairs={{1,0},{0,1},{3,2},{2,3},{5,4},{4,5},{7,6},{6,7},{9,8},{8,9},{11,10... | collective-permute-start | bytes 36872 | tf_op jit(solution)/shard_map/ppermute | solution.py:293
  127.5 18.2 %collective-permute-start.12 = (bf16[512,516]{0,1:T(8,128)(2,1)}, bf16[512,516]{0,1:T(8,128)(2,1)}, u32[]{:S(2)}, u32[]{:S(2)}) collective-permute-start(bf16[512,516]{0,1:T(8,128)(2,1)} %slice.242), channel_id=1, source_target_pairs={{1,0},{0,1},{3,2},{2,3},{5,4},{4,5},{7,6},{6,7},{9,8},{8,9},{11,10... | collective-permute-start | bytes 1585160 | tf_op jit(solution)/shard_map/ppermute | solution.py:293
  129.8 53.6 %collective-permute-start.7 = (bf16[2,256,1024]{2,1,0:T(8,128)(2,1)S(1)}, bf16[2,256,1024]{2,1,0:T(8,128)(2,1)}, u32[]{:S(2)}, u32[]{:S(2)}) collective-permute-start(bf16[2,256,1024]{2,1,0:T(8,128)(2,1)S(1)} %fusion.14), channel_id=1, source_target_pairs={{0,2},{2,0},{4,6},{6,4},{1,3},{3,1},{5,7},{7,5},{8,10},{10,8},{12,... | collective-permute-start | bytes 3145736 | tf_op jit(solution)/shard_map/ppermute | solution.py:309
  131.6 2.0 copy-start.4
  131.6 4.9 %copy-start.21 = (bf16[256,512]{1,0:T(8,128)(2,1)S(1)}, bf16[256,512]{1,0:T(8,128)(2,1)}, u32[]{:S(2)}) copy-start(bf16[256,512]{1,0:T(8,128)(2,1)} %get-tuple-element.64) | copy-start | bytes 786436
  131.6 7.6 %copy-start.22 = (bf16[512,256]{1,0:T(8,128)(2,1)S(1)}, bf16[512,256]{1,0:T(8,128)(2,1)}, u32[]{:S(2)}) copy-start(bf16[512,256]{1,0:T(8,128)(2,1)} %get-tuple-element.66) | copy-start | bytes 786436
  140.3 9.3 %copy-start.20 = (bf16[512,256]{0,1:T(8,128)(2,1)S(1)}, bf16[512,256]{0,1:T(8,128)(2,1)}, u32[]{:S(2)}) copy-start(bf16[512,256]{0,1:T(8,128)(2,1)} %slice.241) | copy-start | bytes 786436
  141.2 12.2 %collective-permute-start.24 = (bf16[512,256]{1,0:T(8,128)(2,1)}, bf16[512,256]{1,0:T(8,128)(2,1)}, u32[]{:S(2)}, u32[]{:S(2)}) collective-permute-start(bf16[512,256]{1,0:T(8,128)(2,1)} %get-tuple-element.54), channel_id=1, source_target_pairs={{0,8},{8,16},{16,24},{24,0},{1,9},{9,17},{17,25},{25,1},{2,10},{10... | collective-permute-start | bytes 786440 | tf_op jit(solution)/shard_map/ppermute | solution.py:383
  142.7 19.2 %collective-permute-start.26 = (bf16[512,256]{1,0:T(8,128)(2,1)}, bf16[512,256]{1,0:T(8,128)(2,1)}, u32[]{:S(2)}, u32[]{:S(2)}) collective-permute-start(bf16[512,256]{1,0:T(8,128)(2,1)} %get-tuple-element.55), channel_id=1, source_target_pairs={{0,24},{8,0},{16,8},{24,16},{1,25},{9,1},{17,9},{25,17},{2,26},{10... | collective-permute-start | bytes 786440 | tf_op jit(solution)/shard_map/ppermute | solution.py:383
  145.0 26.9 %collective-permute-start.25 = (bf16[512,256]{1,0:T(8,128)(2,1)}, bf16[512,256]{1,0:T(8,128)(2,1)}, u32[]{:S(2)}, u32[]{:S(2)}) collective-permute-start(bf16[512,256]{1,0:T(8,128)(2,1)} %get-tuple-element.56), channel_id=1, source_target_pairs={{0,16},{8,24},{16,0},{24,8},{1,17},{9,25},{17,1},{25,9},{2,18},{10... | collective-permute-start | bytes 786440 | tf_op jit(solution)/shard_map/ppermute | solution.py:383
  150.9 31.7 %copy-start.24 = (bf16[2,256]{0,1:T(8,128)(2,1)S(1)}, bf16[2,256]{0,1:T(8,128)(2,1)}, u32[]{:S(2)}) copy-start(bf16[2,256]{0,1:T(8,128)(2,1)} %copy.141) | copy-start | bytes 3076
  152.6 29.9 %collective-permute-start.17 = (bf16[519,256]{0,1:T(8,128)(2,1)}, bf16[519,256]{0,1:T(8,128)(2,1)S(1)}, u32[]{:S(2)}, u32[]{:S(2)}) collective-permute-start(bf16[519,256]{0,1:T(8,128)(2,1)} %pad_maximum_fusion.6), channel_id=1, source_target_pairs={{0,2},{2,0},{4,6},{6,4},{1,3},{3,1},{5,7},{7,5},{8,10},{10,8},{12,... | collective-permute-start | bytes 797192 | tf_op jit(solution)/shard_map/ppermute | solution.py:403
  153.4 20.5 %collective-permute-start.13 = (bf16[272,256]{1,0:T(8,128)(2,1)}, bf16[272,256]{1,0:T(8,128)(2,1)}, u32[]{:S(2)}, u32[]{:S(2)}) collective-permute-start(bf16[272,256]{1,0:T(8,128)(2,1)} %get-tuple-element.61), channel_id=1, source_target_pairs={{0,8},{8,16},{16,24},{24,0},{1,9},{9,17},{17,25},{25,1},{2,10},{10... | collective-permute-start | bytes 417800 | tf_op jit(solution)/shard_map/ppermute | solution.py:383
  161.9 12.1 %collective-permute-start.15 = (bf16[272,256]{1,0:T(8,128)(2,1)}, bf16[272,256]{1,0:T(8,128)(2,1)}, u32[]{:S(2)}, u32[]{:S(2)}) collective-permute-start(bf16[272,256]{1,0:T(8,128)(2,1)} %get-tuple-element.62), channel_id=1, source_target_pairs={{0,24},{8,0},{16,8},{24,16},{1,25},{9,1},{17,9},{25,17},{2,26},{10... | collective-permute-start | bytes 417800 | tf_op jit(solution)/shard_map/ppermute | solution.py:383
  171.9 8.9 %collective-permute-start.14 = (bf16[272,256]{1,0:T(8,128)(2,1)S(1)}, bf16[272,256]{1,0:T(8,128)(2,1)}, u32[]{:S(2)}, u32[]{:S(2)}) collective-permute-start(bf16[272,256]{1,0:T(8,128)(2,1)S(1)} %get-tuple-element.63), channel_id=1, source_target_pairs={{0,16},{8,24},{16,0},{24,8},{1,17},{9,25},{17,1},{25,9},{2,18},{10... | collective-permute-start | bytes 417800 | tf_op jit(solution)/shard_map/ppermute | solution.py:383
  173.9 16.4 %collective-permute-start.3 = (bf16[2,256,1024]{2,1,0:T(8,128)(2,1)}, bf16[2,256,1024]{2,1,0:T(8,128)(2,1)S(1)}, u32[]{:S(2)}, u32[]{:S(2)}) collective-permute-start(bf16[2,256,1024]{2,1,0:T(8,128)(2,1)} %fusion.13), channel_id=1, source_target_pairs={{0,2},{2,0},{4,6},{6,4},{1,3},{3,1},{5,7},{7,5},{8,10},{10,8},{12,... | collective-permute-start | bytes 3145736 | tf_op jit(solution)/shard_map/ppermute | solution.py:309
  182.7 10.6 %collective-permute-start.18 = (bf16[519,256]{0,1:T(8,128)(2,1)S(1)}, bf16[519,256]{0,1:T(8,128)(2,1)S(1)}, u32[]{:S(2)}, u32[]{:S(2)}) collective-permute-start(bf16[519,256]{0,1:T(8,128)(2,1)S(1)} %add_convert_fusion.1), channel_id=1, source_target_pairs={{0,4},{2,6},{4,0},{6,2},{1,5},{3,7},{5,1},{7,3},{8,12},{10,14},{12... | collective-permute-start | bytes 797192 | tf_op jit(solution)/shard_map/ppermute | solution.py:403
  185.6 4.7 %copy-start.5 = (f32[1024,1024]{1,0:T(8,128)S(1)}, f32[1024,1024]{1,0:T(8,128)}, u32[]{:S(2)}) copy-start(f32[1024,1024]{1,0:T(8,128)} %copy-done.4) | copy-start | bytes 12582916
  186.4 46.3 %collective-permute-start.8 = (bf16[256,512]{1,0:T(8,128)(2,1)}, bf16[256,512]{1,0:T(8,128)(2,1)}, u32[]{:S(2)}, u32[]{:S(2)}) collective-permute-start(bf16[256,512]{1,0:T(8,128)(2,1)} %slice.309), channel_id=1, source_target_pairs={{0,1},{1,0},{2,3},{3,2},{4,5},{5,4},{6,7},{7,6},{8,9},{9,8},{10,11... | collective-permute-start | bytes 786440 | tf_op jit(solution)/shard_map/ppermute | solution.py:321
  188.8 45.6 %collective-permute-start.9 = (bf16[256,512]{1,0:T(8,128)(2,1)}, bf16[256,512]{1,0:T(8,128)(2,1)}, u32[]{:S(2)}, u32[]{:S(2)}) collective-permute-start(bf16[256,512]{1,0:T(8,128)(2,1)} %get-tuple-element.68), channel_id=1, source_target_pairs={{0,4},{1,5},{2,6},{3,7},{4,0},{5,1},{6,2},{7,3},{8,12},{9,13},{10,... | collective-permute-start | bytes 786440 | tf_op jit(solution)/shard_map/ppermute | solution.py:321
  194.3 15.3 %copy-start.25 = (bf16[272,256]{1,0:T(8,128)(2,1)S(1)}, bf16[272,256]{1,0:T(8,128)(2,1)}, u32[]{:S(2)}) copy-start(bf16[272,256]{1,0:T(8,128)(2,1)} %fusion.38) | copy-start | bytes 417796
  195.4 8.6 %collective-permute-start.19 = (bf16[144,256]{1,0:T(8,128)(2,1)S(1)}, bf16[144,256]{1,0:T(8,128)(2,1)S(1)}, u32[]{:S(2)}, u32[]{:S(2)}) collective-permute-start(bf16[144,256]{1,0:T(8,128)(2,1)S(1)} %get-tuple-element.78), channel_id=1, source_target_pairs={{0,8},{8,16},{16,24},{24,0},{1,9},{9,17},{17,25},{25,1},{2,10},{10... | collective-permute-start | bytes 221192 | tf_op jit(solution)/shard_map/ppermute | solution.py:383
  195.4 10.0 %collective-permute-start.21 = (bf16[144,256]{1,0:T(8,128)(2,1)S(1)}, bf16[144,256]{1,0:T(8,128)(2,1)S(1)}, u32[]{:S(2)}, u32[]{:S(2)}) collective-permute-start(bf16[144,256]{1,0:T(8,128)(2,1)S(1)} %get-tuple-element.79), channel_id=1, source_target_pairs={{0,24},{8,0},{16,8},{24,16},{1,25},{9,1},{17,9},{25,17},{2,26},{10... | collective-permute-start | bytes 221192 | tf_op jit(solution)/shard_map/ppermute | solution.py:383
  199.2 8.8 %collective-permute-start.20 = (bf16[144,256]{1,0:T(8,128)(2,1)S(1)}, bf16[144,256]{1,0:T(8,128)(2,1)S(1)}, u32[]{:S(2)}, u32[]{:S(2)}) collective-permute-start(bf16[144,256]{1,0:T(8,128)(2,1)S(1)} %get-tuple-element.80), channel_id=1, source_target_pairs={{0,16},{8,24},{16,0},{24,8},{1,17},{9,25},{17,1},{25,9},{2,18},{10... | collective-permute-start | bytes 221192 | tf_op jit(solution)/shard_map/ppermute | solution.py:383
  199.3 10.3 %copy-start.9 = (f32[256,1024]{1,0:T(8,128)}, f32[256,1024]{1,0:T(8,128)S(1)}, u32[]{:S(2)}) copy-start(f32[256,1024]{1,0:T(8,128)S(1)} %dynamic-slice_bitcast_fusion.1) | copy-start | bytes 3145732
  203.9 30.4 %collective-permute-start.10 = (bf16[256,512]{1,0:T(8,128)(2,1)}, bf16[256,512]{1,0:T(8,128)(2,1)S(1)}, u32[]{:S(2)}, u32[]{:S(2)}) collective-permute-start(bf16[256,512]{1,0:T(8,128)(2,1)} %get-tuple-element.69), channel_id=1, source_target_pairs={{0,5},{1,4},{2,7},{3,6},{4,1},{5,0},{6,3},{7,2},{8,13},{9,12},{10,... | collective-permute-start | bytes 786440 | tf_op jit(solution)/shard_map/ppermute | solution.py:321
  205.4 36.6 %collective-permute-start.4 = (bf16[256,512]{1,0:T(8,128)(2,1)}, bf16[256,512]{1,0:T(8,128)(2,1)}, u32[]{:S(2)}, u32[]{:S(2)}) collective-permute-start(bf16[256,512]{1,0:T(8,128)(2,1)} %slice.310), channel_id=1, source_target_pairs={{0,1},{1,0},{2,3},{3,2},{4,5},{5,4},{6,7},{7,6},{8,9},{9,8},{10,11... | collective-permute-start | bytes 786440 | tf_op jit(solution)/shard_map/ppermute | solution.py:321
  208.1 34.0 %collective-permute-start.5 = (bf16[256,512]{1,0:T(8,128)(2,1)}, bf16[256,512]{1,0:T(8,128)(2,1)}, u32[]{:S(2)}, u32[]{:S(2)}) collective-permute-start(bf16[256,512]{1,0:T(8,128)(2,1)} %get-tuple-element.70), channel_id=1, source_target_pairs={{0,4},{1,5},{2,6},{3,7},{4,0},{5,1},{6,2},{7,3},{8,12},{9,13},{10,... | collective-permute-start | bytes 786440 | tf_op jit(solution)/shard_map/ppermute | solution.py:321
  228.1 6.3 %copy-start.6 = (f32[256,1024]{1,0:T(8,128)S(1)}, f32[256,1024]{1,0:T(8,128)}, u32[]{:S(2)}) copy-start(f32[256,1024]{1,0:T(8,128)} %param.18) | copy-start | bytes 3145732
  232.1 7.3 %copy-start.12 = (f32[576,256]{1,0:T(8,128)S(1)}, f32[576,256]{1,0:T(8,128)}, u32[]{:S(2)}) copy-start(f32[576,256]{1,0:T(8,128)} %copy-done.11) | copy-start | bytes 1769476
  232.7 9.3 %collective-permute-start.6 = (bf16[256,512]{1,0:T(8,128)(2,1)}, bf16[256,512]{1,0:T(8,128)(2,1)}, u32[]{:S(2)}, u32[]{:S(2)}) collective-permute-start(bf16[256,512]{1,0:T(8,128)(2,1)} %get-tuple-element.71), channel_id=1, source_target_pairs={{0,5},{1,4},{2,7},{3,6},{4,1},{5,0},{6,3},{7,2},{8,13},{9,12},{10,... | collective-permute-start | bytes 786440 | tf_op jit(solution)/shard_map/ppermute | solution.py:321
  235.7 6.4 %collective-permute-start.11 = (f32[256]{0:T(256)S(1)}, f32[256]{0:T(256)S(1)}, u32[]{:S(2)}, u32[]{:S(2)}) collective-permute-start(f32[256]{0:T(256)S(1)} %multiply_reduce_fusion.6), channel_id=1, source_target_pairs={{1,0},{0,1},{3,2},{2,3},{5,4},{4,5},{7,6},{6,7},{9,8},{8,9},{11,10... | collective-permute-start | bytes 3080 | tf_op jit(solution)/shard_map/ppermute | solution.py:293
  240.9 1.7 copy-start.16
  (6 other events, 7.4 us)
Sparse Core Ops, SparseCore 0:
  11.9 25.2 all-gather.5
  48.3 23.7 all-gather.7
  174.0 32.5 all-gather.9
